TPU v7x, 256 devices: a whole 4x4x8 slice. The times are simulated.
256 devices in a mesh: samp: 16 (over z, core), feat: 16 (over x, y).
Axes of the slice: x: 4, y: 4, z: 8, core: 2. Of those that a mesh axis runs over, the one named last changes fastest.
Arguments:
- differences: bfloat16 [9216, 131072], P('samp', 'feat'), may hold values from -600 to 600
- start_block: bfloat16 [64, 131072], P(None, 'feat'), may hold values from -6 to 6
Outputs:
- directions: float32 [64, 131072], P(None, 'feat')
- layer_scores: float32 [16, 64], P('feat')
All inputs are finite; a program needn't handle non-finite values.
Results may differ from a plain program's by a relative error of at most 0.0043.
Values may be sent and summed in bfloat16 or wider, within the bound.
A program may use at most 64 MiB of HBM per device.

v0:
```python
import math

import jax
import jax.numpy as jnp
from jax import lax
from jax.sharding import PartitionSpec as P

WIDTH = 8192
ITERS = 2
FEATURES = 131072


def orthonormal(pulled, gram):
    lower = jnp.linalg.cholesky(gram)
    return lax.linalg.triangular_solve(lower, pulled, left_side=True, lower=True)


def on_device(differences, start_block):
    block = start_block
    basis = None
    for step in range(ITERS):
        partial_rows = lax.dot_general(
            block, differences, (((1,), (1,)), ((), ())), preferred_element_type=jnp.float32
        )
        projected = lax.psum(partial_rows, "feat").astype(jnp.bfloat16)
        partial_cols = jnp.dot(projected, differences, preferred_element_type=jnp.float32)
        pulled = lax.psum(partial_cols, "samp")
        local_gram = jnp.dot(pulled, pulled.T, precision=lax.Precision.HIGHEST)
        gram = lax.psum(local_gram, "feat")
        basis = orthonormal(pulled, gram)
        block = basis.astype(jnp.bfloat16)
    directions = basis * math.sqrt(FEATURES)
    samples = differences.shape[0]
    layers_here = differences.shape[1] // WIDTH
    stacked = differences.reshape(samples, layers_here, WIDTH)
    block_layers = block.reshape(block.shape[0], layers_here, WIDTH)
    along = jnp.einsum("kjw,sjw->jks", block_layers, stacked, preferred_element_type=jnp.float32)
    captured = jnp.sum(along * along, axis=2)
    energy = jnp.einsum("sjw,sjw->j", stacked, stacked, preferred_element_type=jnp.float32)
    captured, energy = lax.psum((captured, energy), "samp")
    layer_scores = FEATURES * captured / (energy[:, None] + 1e-06)
    return (directions, layer_scores)


def solution(mesh):
    in_specs = (P("samp", "feat"), P(None, "feat"))
    out_specs = (P(None, "feat"), P("feat", None))
    return jax.shard_map(
        on_device, mesh=mesh, in_specs=in_specs, out_specs=out_specs, check_vma=False
    )
```

profile of v0, /device:TPU:1, one launch (start us, length us, event | category | flops | bytes accessed | tf_op | source)
XLA Modules:
  0.0 635.0 jit_solution(9600654586622632830)
XLA Ops:
  7.2 1.2 copy-done
  8.4 6.6 %fusion.16 = f32[64,576]{1,0:T(8,128)S(1)} fusion(bf16[64,8192]{1,0:T(8,128)(2,1)S(1)} %copy-done, bf16[576,8192]{1,0:T(8,128)(2,1)} %param.5), kind=kOutput, calls=%fused_computation.30 | convolution fusion | flops 603979776 | bytes 10633216 | tf_op jit(solution)/shard_map/dot_general | solution.py:22
  15.0 63.0 %all-reduce.9 = bf16[64,576]{1,0:T(8,128)(2,1)S(1)} all-reduce(f32[64,576]{1,0:T(8,128)S(1)} %fusion.16), channel_id=1, replica_groups=mesh['samp'=16,'feat'=16] {'feat'}, use_global_device_ids=true, to_apply=%region_0.0 | all-reduce | flops 36864 | bytes 221184 | tf_op jit(solution)/shard_map/psum | solution.py:25
  77.9 6.9 %fusion.21 = f32[64,8192]{1,0:T(8,128)} fusion(bf16[64,576]{1,0:T(8,128)(2,1)S(1)} %all-reduce.9, bf16[576,8192]{1,0:T(8,128)(2,1)} %param.5), kind=kOutput, calls=%fused_computation.35 | convolution fusion | flops 603979776 | bytes 11608064 | tf_op jit(solution)/shard_map/dot_general | solution.py:26
  84.9 127.8 %all-reduce.6.cloned.1.call-done = f32[64,8192]{1,0:T(8,128)} async-done(((f32[64,8192]{1,0:T(8,128)}), f32[64,8192]{1,0:T(8,128)}) %all-reduce.6.cloned.1.call-update) | async-done | bytes 2097168 | tf_op jit(solution)/shard_map/psum | solution.py:27
  212.7 4.2 fusion.17
  216.9 60.3 %psum.58 = f32[64,64]{0,1:T(8,128)S(1)} all-reduce(f32[64,64]{0,1:T(8,128)S(1)} %fusion.17), channel_id=1, replica_groups=mesh['samp'=16,'feat'=16] {'feat'}, use_global_device_ids=true, to_apply=%region_2.0 | all-reduce | flops 4096 | bytes 32768 | tf_op jit(solution)/shard_map/psum | solution.py:29
  277.2 5.8 cholesky.44
  283.8 0.7 fusion.7
  284.4 4.9 custom-call.6
  289.3 1.9 convolution_convert_fusion
  291.2 6.6 %fusion.18 = f32[64,576]{1,0:T(8,128)S(1)} fusion(bf16[64,8192]{1,0:T(8,128)(2,1)S(1)} %convolution_convert_fusion, bf16[576,8192]{1,0:T(8,128)(2,1)} %param.5), kind=kOutput, calls=%fused_computation.32 | convolution fusion | flops 603979776 | bytes 10633216 | tf_op jit(solution)/shard_map/dot_general | solution.py:22
  297.8 57.4 %all-reduce.10 = bf16[64,576]{1,0:T(8,128)(2,1)S(1)} all-reduce(f32[64,576]{1,0:T(8,128)S(1)} %fusion.18), channel_id=1, replica_groups=mesh['samp'=16,'feat'=16] {'feat'}, use_global_device_ids=true, to_apply=%region_5.8 | all-reduce | flops 36864 | bytes 221184 | tf_op jit(solution)/shard_map/psum | solution.py:25
  355.3 6.9 %fusion.20 = f32[64,8192]{1,0:T(8,128)} fusion(bf16[64,576]{1,0:T(8,128)(2,1)S(1)} %all-reduce.10, bf16[576,8192]{1,0:T(8,128)(2,1)} %param.5), kind=kOutput, calls=%fused_computation.34 | convolution fusion | flops 603979776 | bytes 11608064 | tf_op jit(solution)/shard_map/dot_general | solution.py:26
  362.2 9.1 %fusion = f32[]{:T(128)} fusion(bf16[576,8192]{1,0:T(8,128)(2,1)} %param.5), kind=kLoop, calls=%fused_computation.1 | loop fusion | flops 14155775 | bytes 9437188 | tf_op jit(solution)/shard_map/sjw,sjw->j/dot_general | solution.py:39
  371.4 130.6 %all-reduce.8.cloned.1.call-done = f32[64,8192]{1,0:T(8,128)} async-done(((f32[64,8192]{1,0:T(8,128)}), f32[64,8192]{1,0:T(8,128)}) %all-reduce.8.cloned.1.call-update) | async-done | bytes 2097168 | tf_op jit(solution)/shard_map/psum | solution.py:27
  502.0 4.2 fusion.19
  506.1 60.3 %psum.61 = f32[64,64]{0,1:T(8,128)S(1)} all-reduce(f32[64,64]{0,1:T(8,128)S(1)} %fusion.19), channel_id=1, replica_groups=mesh['samp'=16,'feat'=16] {'feat'}, use_global_device_ids=true, to_apply=%region_7.10 | all-reduce | flops 4096 | bytes 32768 | tf_op jit(solution)/shard_map/psum | solution.py:29
  566.5 5.8 cholesky.55
  573.0 0.7 fusion.8
  573.7 4.9 custom-call.7
  578.6 3.3 broadcast_multiply_fusion
  581.9 6.7 %fusion.1 = f32[64]{0:T(128)S(1)} fusion(bf16[576,8192]{1,0:T(8,128)(2,1)} %param.5, bf16[64,8192]{1,0:T(8,128)(2,1)S(1)} %get-tuple-element.7), kind=kOutput, calls=%fused_computation.4 | convolution fusion | flops 604053440 | bytes 10486016 | tf_op jit(solution)/shard_map/kjw,sjw->jks/dot_general | solution.py:37
  588.6 38.4 %all-reduce = (f32[1,64]{1,0:T(1,128)S(1)}, f32[1]{0:T(128)}) all-reduce(f32[1,64]{1,0:T(1,128)S(1)} %bitcast.39, f32[1]{0:T(128)} %bitcast.7), channel_id=1, replica_groups=mesh['samp'=16,'feat'=16] {'samp'}, use_global_device_ids=true, to_apply=%region_9.12 | all-reduce | flops 65 | bytes 520 | tf_op jit(solution)/shard_map/psum | solution.py:40
  (18 shorter events, 2.2 us)
Async XLA Ops:
  7.2 1.2 copy-start
  7.2 205.5 %all-reduce.6.cloned.1.call-start = ((), (), s32[]{:S(2)}) async-start(), calls=%async_computation | async-start | bytes 4194304 | tf_op jit(solution)/shard_map/psum | solution.py:27
  84.9 417.1 %all-reduce.8.cloned.1.call-start = ((), (), s32[]{:S(2)}) async-start(), calls=%async_computation.1 | async-start | bytes 4194304 | tf_op jit(solution)/shard_map/psum | solution.py:27
  212.7 76.6 %copy-start.2 = (f32[64,8192]{1,0:T(8,128)S(1)}, f32[64,8192]{1,0:T(8,128)}, u32[]{:S(2)}) copy-start(f32[64,8192]{1,0:T(8,128)} %all-reduce.6.cloned.1.call-done) | copy-start | bytes 6291460
  502.0 76.6 %copy-start.1 = (f32[64,8192]{1,0:T(8,128)S(1)}, f32[64,8192]{1,0:T(8,128)}, u32[]{:S(2)}) copy-start(f32[64,8192]{1,0:T(8,128)} %all-reduce.8.cloned.1.call-done) | copy-start | bytes 6291460
Sparse Core Ops, SparseCore 0:
  85.0 127.6 all-reduce.5
  362.3 139.5 all-reduce.7
where the time goes:
time: 635 us
  blocking collectives  279 us (44%)
  waiting for transfers between devices  258 us (41%)
  matrix products  47.2 us (7%)
  other arithmetic  33.8 us (5%)
  between operations  14.8 us (2%)
    psum x2, waiting for transfers between devices, on_device(): pulled = lax.psum(partial_cols, 'samp')  258 us
    psum x2, blocking collectives, on_device(): gram = lax.psum(local_gram, 'feat')  121 us
    psum x2, blocking collectives, on_device(): projected = lax.psum(partial_rows, 'feat').astype(jnp.bfloat16)  120 us
    psum x1, blocking collectives, on_device(): captured, energy = lax.psum((captured, energy), 'samp')  38.4 us
    dot_general x2, matrix products, on_device(): jnp.dot(projected, differences, preferred_element_type=jnp.float32)  13.8 us
    dot_general x2, matrix products, on_device(): lax.dot_general(block, differences, (((1,), (1,)), ((), ())), preferred_e...  13.2 us
    another operation x6, other arithmetic, orthonormal(): lower = jnp.linalg.cholesky(gram)  13 us
  transfers between devices with their start and end apart: 2, of which 2 were waited for; matrix products, arithmetic and copies ran while one was open for 1% of the time, Pallas kernels for 0%

commit v1 on v0

v1 whole, which is shorter than its diff:
```python
import functools
import math

import jax
import jax.numpy as jnp
from jax import lax
from jax.experimental import pallas as pl
from jax.experimental.pallas import tpu as pltpu
from jax.sharding import PartitionSpec as P

FEATURES = 131072
K = 64
NS = 576
WF = 8192
NP = 16
PW = WF // NP
HALF = PW // 2
ROWS = K // 16
WQ = NS + K
MESH = pl.DeviceIdType.MESH
F32 = jnp.float32
BF16 = jnp.bfloat16


def dot_nn(a, b):
    return lax.dot_general(a, b, (((1,), (0,)), ((), ())), preferred_element_type=F32)


def dot_nt(a, b):
    return lax.dot_general(a, b, (((1,), (1,)), ((), ())), preferred_element_type=F32)


def dot_exact(a, b):
    return lax.dot_general(a, b, (((1,), (0,)), ((), ())), preferred_element_type=F32, precision=lax.Precision.HIGHEST)


def inverse_factor(gram):
    row = lax.broadcasted_iota(jnp.int32, (K, K), 0)
    col = lax.broadcasted_iota(jnp.int32, (K, K), 1)
    m = jnp.concatenate([gram, jnp.where(row == col, 1.0, 0.0).astype(F32)], axis=1)
    below = lax.broadcasted_iota(jnp.int32, (K, 1), 0)
    scale = jnp.zeros((K, 1), F32)
    for j in range(K):
        pivot_row = m[j:j + 1, :]
        d = pivot_row[:, j:j + 1]
        scale = jnp.where(below == j, d, scale)
        if j < K - 1:
            factor = jnp.where(below > j, m[:, j:j + 1] * (1.0 / d), 0.0)
            m = m - factor * pivot_row
    inv = lax.rsqrt(scale)
    inv = inv * (1.5 - 0.5 * ((scale * inv) * inv))
    return m[:, K:] * inv


def kernel(d_hbm, s_hbm, dir_hbm, score_ref,
           dv, sv, x2, psend, precv, rs_s, rs_r, ls_s, ls_r, r0_s, r0_r, l0_s, l0_r, acc,
           qs, qr, qo, qg, qf, hs, hr, ho, hg, hf, fs, dout,
           d_sem, s_sem, o_sem, ar_s, ar_r, pair_s, pair_r, rr_s, rr_r, rl_s, rl_r,
           ag_rs, ag_rr, ag_ls, ag_lr, sib_s, sib_r, f_s, f_r):
    samp = lax.axis_index("samp")
    feat = lax.axis_index("feat")
    z = samp // 2
    c = samp % 2
    right = (((z + 1) % 8) * 2 + c, feat)
    left = (((z + 7) % 8) * 2 + c, feat)
    sibling = (z * 2 + (1 - c), feat)
    pending = []

    def send(src, dst, ssem, rsem, dev):
        copy = pltpu.make_async_remote_copy(src_ref=src, dst_ref=dst, send_sem=ssem, recv_sem=rsem,
                                            device_id=dev, device_id_type=MESH)
        copy.start()
        pending.append(copy)
        return copy

    barrier = pltpu.get_barrier_semaphore()
    for r in range(1, 16):
        pl.semaphore_signal(barrier, inc=1, device_id=(samp, (feat + r) % 16), device_id_type=MESH)
        pl.semaphore_signal(barrier, inc=1, device_id=((samp + r) % 16, feat), device_id_type=MESH)

    d_copies = []
    for p in range(NP):
        dc = pltpu.make_async_copy(d_hbm.at[:, p * PW:(p + 1) * PW], dv.at[p, 0:NS, :], d_sem.at[p])
        sc = pltpu.make_async_copy(s_hbm.at[:, p * PW:(p + 1) * PW], sv.at[p], s_sem.at[p])
        sc.start()
        dc.start()
        d_copies.append((dc, sc))

    def all_reduce(it, parts, arrived, own, gathered, full):
        copies = []
        for r in range(1, 16):
            copies.append(send(parts.at[(feat + r) % 16], arrived.at[r], ar_s.at[it, 0, r], ar_r.at[it, 0, r],
                               (samp, (feat + r) % 16)))
        yield
        total = parts[feat]
        for r in range(1, 16):
            copies[r - 1].wait_recv()
            total = total + arrived[r]
        own[...] = total
        copies = []
        for r in range(1, 16):
            copies.append(send(own, gathered.at[r], ar_s.at[it, 1, r], ar_r.at[it, 1, r],
                               (samp, (feat + r) % 16)))
        gathered[0] = total
        yield
        for r in range(1, 16):
            copies[r - 1].wait_recv()
        for j in range(16):
            full[j * ROWS:(j + 1) * ROWS, :] = gathered[(feat - j + 16) % 16]
        yield

    def split(value, parts):
        for j in range(16):
            parts[j] = value[j * ROWS:(j + 1) * ROWS, :]

    q = jnp.zeros((K, NS), F32)
    for p in range(NP):
        dc, sc = d_copies[p]
        sc.wait()
        dc.wait()
        q = q + dot_nt(sv[p], dv[p, 0:NS, :])
    split(jnp.concatenate([q, jnp.zeros((K, K), F32)], axis=1), qs.at[0])
    pl.semaphore_wait(barrier, 30)
    reduce = all_reduce(0, qs.at[0], qr.at[0], qo.at[0], qg.at[0], qf.at[0])
    next(reduce)

    def energy_step(p, total):
        wide = dv[p, 0:NS, :].astype(F32)
        return total + jnp.sum(wide * wide, axis=0, keepdims=True)

    energy = lax.fori_loop(0, NP, energy_step, jnp.zeros((1, PW), F32))
    energy = jnp.sum(energy, axis=1, keepdims=True)
    next(reduce)
    next(reduce)
    projected = qf[0, :, 0:NS].astype(BF16)

    def pull_and_scatter(it, projected):
        pair = {}

        def compute(d):
            there = (z + d) % 8
            psend[it, d] = dot_nn(projected, dv[(1 - c) * 8 + there, 0:NS, :]).astype(BF16)
            pair[d] = send(psend.at[it, d], precv.at[it, d], pair_s.at[it, d], pair_r.at[it, d], sibling)
            acc[d] = dot_nn(projected, dv[c * 8 + there, 0:NS, :])

        def both(d):
            pair[d].wait_recv()
            return acc[d] + precv[it, d].astype(F32)

        compute(4)
        compute(3)
        compute(5)
        far = both(4)
        r0_s[it] = far[:, 0:HALF].astype(BF16)
        l0_s[it] = far[:, HALF:].astype(BF16)
        to_right = send(r0_s.at[it], r0_r.at[it], rr_s.at[it, 0], rr_r.at[it, 0], right)
        to_left = send(l0_s.at[it], l0_r.at[it], rl_s.at[it, 0], rl_r.at[it, 0], left)
        compute(2)
        for t in range(1, 4):
            part = both(4 - t)
            to_right.wait_recv()
            if t == 1:
                rs_s[it, t, :, 0:HALF] = (part[:, 0:HALF] + r0_r[it].astype(F32)).astype(BF16)
                rs_s[it, t, :, HALF:] = part[:, HALF:].astype(BF16)
            else:
                rs_s[it, t] = (part + rs_r[it, t - 1].astype(F32)).astype(BF16)
            to_right = send(rs_s.at[it, t], rs_r.at[it, t], rr_s.at[it, t], rr_r.at[it, t], right)
            part = both(4 + t)
            to_left.wait_recv()
            if t == 1:
                ls_s[it, t, :, 0:HALF] = part[:, 0:HALF].astype(BF16)
                ls_s[it, t, :, HALF:] = (part[:, HALF:] + l0_r[it].astype(F32)).astype(BF16)
            else:
                ls_s[it, t] = (part + ls_r[it, t - 1].astype(F32)).astype(BF16)
            to_left = send(ls_s.at[it, t], ls_r.at[it, t], rl_s.at[it, t], rl_r.at[it, t], left)
            if t == 1:
                compute(6)
                compute(1)
            elif t == 2:
                compute(7)
                compute(0)
        part = both(0)
        to_right.wait_recv()
        to_left.wait_recv()
        return (part + rs_r[it, 3].astype(F32) + ls_r[it, 3].astype(F32)).astype(BF16)

    def gather(it, slot, use):
        here = c * 8
        there = (1 - c) * 8

        def to_sibling(d):
            p = here + (z + d) % 8
            return send(slot(p), slot(p), sib_s.at[it, d], sib_r.at[it, d], sibling)

        def ring(t, d, cols, sems, dev):
            p = here + (z + d) % 8
            src = slot(p) if cols is None else slot(p).at[:, cols]
            return send(src, src, sems[0].at[it, t], sems[1].at[it, t], dev)

        rsem = (ag_rs, ag_rr)
        lsem = (ag_ls, ag_lr)
        sib = {}
        to_right = ring(1, 0, None, rsem, right)
        to_left = ring(1, 0, None, lsem, left)
        sib[0] = to_sibling(0)
        use(here + z)
        for t in range(1, 4):
            nxt = None if t < 3 else True
            to_right.wait_recv()
            to_right = ring(t + 1, 8 - t, None if t < 3 else slice(0, HALF), rsem, right)
            sib[8 - t] = to_sibling(8 - t)
            to_left.wait_recv()
            to_left = ring(t + 1, t, None if t < 3 else slice(HALF, PW), lsem, left)
            sib[t] = to_sibling(t)
            if t == 1:
                sib[0].wait_recv()
                use(there + z)
            else:
                sib[9 - t].wait_recv()
                use(there + (z + 9 - t) % 8)
                sib[t - 1].wait_recv()
                use(there + (z + t - 1) % 8)
            use(here + (z + 8 - t) % 8)
            use(here + (z + t) % 8)
        to_right.wait_recv()
        to_left.wait_recv()
        sib[4] = to_sibling(4)
        use(here + (z + 4) % 8)
        sib[5].wait_recv()
        use(there + (z + 5) % 8)
        sib[3].wait_recv()
        use(there + (z + 3) % 8)
        sib[4].wait_recv()
        use(there + (z + 4) % 8)

    piece = pull_and_scatter(0, projected)
    dv[samp_piece(z, c), NS:, :] = piece
    qf[1] = jnp.zeros((K, WQ), F32)

    def use_first(p):
        qf[1] += dot_nt(dv[p, NS:, :], dv[p])

    gather(0, lambda p: dv.at[p, NS:, :], use_first)
    split(qf[1], qs.at[1])
    reduce = all_reduce(1, qs.at[1], qr.at[1], qo.at[1], qg.at[1], qf.at[2])
    next(reduce)
    next(reduce)
    next(reduce)
    inv = inverse_factor(qf[2, :, NS:])
    projected = dot_exact(inv, qf[2, :, 0:NS]).astype(BF16)

    piece = pull_and_scatter(1, projected)
    x2[samp_piece(z, c)] = piece
    qf[3] = jnp.zeros((K, WQ), F32)
    hf[0] = jnp.zeros((K, 128), F32)

    def use_second(p):
        x = x2[p]
        qf[3, :, 0:NS] += dot_nt(x, dv[p, 0:NS, :])
        hf[0, :, 0:K] += dot_nt(x, x)

    gather(1, lambda p: x2.at[p], use_second)
    split(hf[0], hs)
    reduce = all_reduce(2, hs, hr, ho, hg, hf.at[1])
    next(reduce)
    next(reduce)
    next(reduce)
    inv = inverse_factor(hf[1, :, 0:K])
    along = dot_exact(inv, qf[3, :, 0:NS])
    captured = lax.dot_general(jnp.ones((8, NS), F32), along * along, (((1,), (1,)), ((), ())),
                               preferred_element_type=F32, precision=lax.Precision.HIGHEST)
    fs[samp] = jnp.concatenate([captured, jnp.broadcast_to(energy, (8, K))], axis=1)
    last = []
    for r in range(1, 16):
        last.append(send(fs.at[samp], fs.at[samp], f_s.at[r], f_r.at[r], ((samp + r) % 16, feat)))

    scaled = inv * math.sqrt(FEATURES)
    high = scaled.astype(BF16)
    low = (scaled - high.astype(F32)).astype(BF16)
    stacked = jnp.concatenate([high, low], axis=0)
    outs = []
    for p in range(NP):
        both = dot_nn(stacked, x2[p])
        dout[p] = both[0:K] + both[K:]
        oc = pltpu.make_async_copy(dout.at[p], dir_hbm.at[:, p * PW:(p + 1) * PW], o_sem.at[p])
        oc.start()
        outs.append(oc)
    for copy in last:
        copy.wait_recv()
    total = fs[0]
    for r in range(1, 16):
        total = total + fs[r]
    score_ref[...] = FEATURES * total[:, 0:K] / (total[:, K:] + 1e-6)
    for oc in outs:
        oc.wait()
    for copy in pending:
        copy.wait_send()


def samp_piece(z, c):
    return c * 8 + z


def on_device(differences, start_block):
    dma = pltpu.SemaphoreType.DMA
    directions, scores = pl.pallas_call(
        kernel,
        out_shape=(jax.ShapeDtypeStruct((K, WF), F32), jax.ShapeDtypeStruct((8, K), F32)),
        in_specs=[pl.BlockSpec(memory_space=pl.ANY), pl.BlockSpec(memory_space=pl.ANY)],
        out_specs=(pl.BlockSpec(memory_space=pl.ANY), pl.BlockSpec(memory_space=pltpu.VMEM)),
        scratch_shapes=[
            pltpu.VMEM((NP, WQ, PW), BF16),
            pltpu.VMEM((NP, K, PW), BF16),
            pltpu.VMEM((NP, K, PW), BF16),
            pltpu.VMEM((2, 8, K, PW), BF16),
            pltpu.VMEM((2, 8, K, PW), BF16),
            pltpu.VMEM((2, 4, K, PW), BF16),
            pltpu.VMEM((2, 4, K, PW), BF16),
            pltpu.VMEM((2, 4, K, PW), BF16),
            pltpu.VMEM((2, 4, K, PW), BF16),
            pltpu.VMEM((2, K, HALF), BF16),
            pltpu.VMEM((2, K, HALF), BF16),
            pltpu.VMEM((2, K, HALF), BF16),
            pltpu.VMEM((2, K, HALF), BF16),
            pltpu.VMEM((8, K, PW), F32),
            pltpu.VMEM((2, 16, ROWS, WQ), F32),
            pltpu.VMEM((2, 16, ROWS, WQ), F32),
            pltpu.VMEM((2, ROWS, WQ), F32),
            pltpu.VMEM((2, 16, ROWS, WQ), F32),
            pltpu.VMEM((4, K, WQ), F32),
            pltpu.VMEM((16, ROWS, 128), F32),
            pltpu.VMEM((16, ROWS, 128), F32),
            pltpu.VMEM((ROWS, 128), F32),
            pltpu.VMEM((16, ROWS, 128), F32),
            pltpu.VMEM((2, K, 128), F32),
            pltpu.VMEM((16, 8, 128), F32),
            pltpu.VMEM((NP, K, PW), F32),
            dma((NP,)), dma((NP,)), dma((NP,)),
            dma((3, 2, 16)), dma((3, 2, 16)),
            dma((2, 8)), dma((2, 8)),
            dma((2, 4)), dma((2, 4)), dma((2, 4)), dma((2, 4)),
            dma((2, 5)), dma((2, 5)), dma((2, 5)), dma((2, 5)),
            dma((2, 8)), dma((2, 8)),
            dma((16,)), dma((16,)),
        ],
        compiler_params=pltpu.CompilerParams(collective_id=0, has_side_effects=True, vmem_limit_bytes=48 * 1024 * 1024),
    )(differences, start_block)
    return directions, scores[0:1]


def solution(mesh):
    in_specs = (P("samp", "feat"), P(None, "feat"))
    out_specs = (P(None, "feat"), P("feat", None))
    return jax.shard_map(
        on_device, mesh=mesh, in_specs=in_specs, out_specs=out_specs, check_vma=False
    )
```

time: 635 us -> 130 us (0.20)
  blocking collectives: 279 us -> 0 us
  waiting for transfers between devices: 258 us -> 0 us
  Pallas kernels: 0 us -> 127 us
  matrix products: 47.2 us -> 0 us
  other arithmetic: 33.8 us -> 0 us
  between operations: 14.8 us -> 0.65 us
    psum x5 -> x0, blocking collectives: 279 us -> none  [the longest x2 121 us: on_device(): gram = lax.psum(local_gram, 'feat')]
    psum x2 -> x0, waiting for transfers between devices: 258 us -> none  [on_device(): pulled = lax.psum(partial_cols, 'samp')]
    pallas_call x0 -> x1, Pallas kernels: none -> 127 us  [on_device(): pl.pallas_call(kernel, out_shape=(jax.ShapeDtypeStruct((K, WF), F32), jax...]
    dot_general x7 -> x0, matrix products: 42 us -> none  [the longest x2 13.8 us: on_device(): jnp.dot(projected, differences, preferred_element_type=jnp.float32)]
    another operation x10 -> x0, other arithmetic: 24.1 us -> none  [the longest x6 13 us: orthonormal(): lower = jnp.linalg.cholesky(gram)]
    dot_general x1 -> x0, other arithmetic: 9.15 us -> none  [on_device(): jnp.einsum('sjw,sjw->j', stacked, stacked, preferred_element_type=jnp.flo...]
  transfers between devices with their start and end apart: 2 -> 0, of which waited for: 2 -> 0; matrix products, arithmetic and copies ran while one was open for 1% -> 0% of each run, Pallas kernels for 0% -> 0%
where the time goes in v1:
time: 130 us
  Pallas kernels  127 us (98%)
  local copies, waits for them, and re-layouts  3.05 us (2%)
    pallas_call x1, Pallas kernels, on_device(): pl.pallas_call(kernel, out_shape=(jax.ShapeDtypeStruct((K, WF), F32), jax...  127 us

profile of v1, /device:TPU:1, one launch (start us, length us, event | category | flops | bytes accessed | tf_op | source)
XLA Modules:
  0.0 130.3 jit_solution(10488626598546499945)
XLA Ops:
  0.6 0.0 copy-start
  0.6 1.2 copy-done
  1.9 126.6 %shard_map.41 = (f32[64,8192]{1,0:T(8,128)S(1)}, f32[8,64]{1,0:T(8,128)S(1)}) custom-call(bf16[576,8192]{1,0:T(8,128)(2,1)} %d_hbm.1, bf16[64,8192]{1,0:T(8,128)(2,1)S(1)} %copy-done), custom_call_target="tpu_custom_call" | custom-call | tf_op jit(solution)/shard_map/pallas_call | solution.py:306
  128.5 0.5 slice.3
  129.0 1.3 %copy.5 = f32[64,8192]{1,0:T(8,128)} copy(f32[64,8192]{1,0:T(8,128)S(1)} %get-tuple-element.8) | data formatting | bytes 4194304
Async XLA Ops:
  0.6 1.2 copy-start

commit v2 on v0

v2 whole, which is shorter than its diff:
```python
import math

import jax
import jax.numpy as jnp
from jax import lax
from jax.experimental import pallas as pl
from jax.experimental.pallas import tpu as pltpu
from jax.sharding import PartitionSpec as P

FEATURES = 131072
K = 64
NS = 576
WF = 8192
NP = 16
PW = WF // NP
HALF = PW // 2
ROWS = K // 16
WQ = NS + K
MESH = pl.DeviceIdType.MESH
F32 = jnp.float32
BF16 = jnp.bfloat16


def dot_nn(a, b):
    return lax.dot_general(a, b, (((1,), (0,)), ((), ())), preferred_element_type=F32)


def dot_nt(a, b):
    return lax.dot_general(a, b, (((1,), (1,)), ((), ())), preferred_element_type=F32)


def dot_exact(a, b):
    return lax.dot_general(a, b, (((1,), (0,)), ((), ())), preferred_element_type=F32, precision=lax.Precision.HIGHEST)


def inverse_factor(gram):
    row = lax.broadcasted_iota(jnp.int32, (8, 2 * K), 0)
    col = lax.broadcasted_iota(jnp.int32, (8, 2 * K), 1)
    wide = jnp.concatenate([gram, jnp.zeros((K, K), F32)], axis=1)
    m = [wide[8 * g:8 * g + 8, :] + jnp.where(col == row + (K + 8 * g), 1.0, 0.0) for g in range(8)]
    out = []
    for b in range(8):
        cols = [[jnp.broadcast_to(m[g][:, 8 * b + k:8 * b + k + 1], (8, 2 * K)) for k in range(8)] for g in range(b, 8)]
        diag = jnp.zeros((8, 2 * K), F32)
        for k in range(8):
            d = cols[0][k][k:k + 1, :]
            r = 1.0 / d
            diag = jnp.where(row == k, d, diag)
            pivot_row = m[b][k:k + 1, :] * r
            factor = [jnp.where(row > k, cols[0][k], 0.0)] + [cols[i][k] for i in range(1, 8 - b)]
            for i in range(8 - b):
                m[b + i] = m[b + i] - factor[i] * pivot_row
            for kk in range(k + 1, 8):
                t = cols[0][k][kk:kk + 1, :] * r
                for i in range(8 - b):
                    cols[i][kk] = cols[i][kk] - factor[i] * t
        inv = lax.rsqrt(diag)
        inv = inv * (1.5 - 0.5 * ((diag * inv) * inv))
        out.append((m[b] * inv)[:, K:])
    return jnp.concatenate(out, axis=0)


def pack(square):
    return jnp.concatenate([square[0:K // 2], square[K // 2:]], axis=1)


def unpack(wide):
    return jnp.concatenate([wide[:, 0:K], wide[:, K:]], axis=0)


def ring_hops(d, n):
    return min(d, n - d)


PLANE = sorted([(dx, dy) for dx in range(4) for dy in range(4) if dx or dy],
               key=lambda o: -(ring_hops(o[0], 4) + ring_hops(o[1], 4)))
COLUMN = [4, 3, 5, 2, 6, 1, 7]


def kernel(d_hbm, s_hbm, dir_hbm, score_ref,
           dv, sv, x2, psend, precv, msg_s, msg_r, half_s, half_r, acc,
           qs, qr, qo, qg, qf, gg, es, cs, cr, cg, dout,
           d_sem, s_sem, o_sem, ar_s, ar_r, pair_s, pair_r, rs_s, rs_r,
           ag_s, ag_r, sib_s, sib_r, g_s, g_r, e_s, e_r, c_s, c_r):
    samp = lax.axis_index("samp")
    feat = lax.axis_index("feat")
    z = samp // 2
    c = samp % 2
    x = feat // 4
    y = feat % 4
    sibling = (z * 2 + (1 - c), feat)
    pending = []

    def chip(d):
        return (((z + d) % 8) * 2 + c, feat)

    def across(dx, dy):
        return ((x + dx) % 4) * 4 + (y + dy) % 4

    def send(src, dst, ssem, rsem, dev):
        copy = pltpu.make_async_remote_copy(src_ref=src, dst_ref=dst, send_sem=ssem, recv_sem=rsem,
                                            device_id=dev, device_id_type=MESH)
        copy.start()
        pending.append(copy)
        return copy

    barrier = pltpu.get_barrier_semaphore()
    for r in range(1, 16):
        pl.semaphore_signal(barrier, inc=1, device_id=(samp, (feat + r) % 16), device_id_type=MESH)
        pl.semaphore_signal(barrier, inc=1, device_id=((samp + r) % 16, feat), device_id_type=MESH)

    d_copies = []
    for p in range(NP):
        dc = pltpu.make_async_copy(d_hbm.at[:, p * PW:(p + 1) * PW], dv.at[p, 0:NS, :], d_sem.at[p])
        sc = pltpu.make_async_copy(s_hbm.at[:, p * PW:(p + 1) * PW], sv.at[p], s_sem.at[p])
        sc.start()
        dc.start()
        d_copies.append((dc, sc))

    def reduce_scatter_q(it, value):
        for j in range(16):
            qs[it, j] = value[j * ROWS:(j + 1) * ROWS, :]
        copies = []
        for dx, dy in PLANE:
            r = dx * 4 + dy
            there = across(dx, dy)
            copies.append((r, send(qs.at[it, there], qr.at[it, r], ar_s.at[it, 0, r], ar_r.at[it, 0, r], (samp, there))))
        return copies

    def gather_q(it, copies):
        total = qs[it, feat]
        for r, copy in copies:
            copy.wait_recv()
            total = total + qr[it, r]
        qo[it] = total
        qg[it, 0] = total
        copies = []
        for dx, dy in PLANE:
            r = dx * 4 + dy
            copies.append(send(qo.at[it], qg.at[it, r], ar_s.at[it, 1, r], ar_r.at[it, 1, r], (samp, across(dx, dy))))
        return copies

    def join_q(it, copies):
        for copy in copies:
            copy.wait_recv()
        for j in range(16):
            slot = ((x - j // 4 + 4) % 4) * 4 + (y - j % 4 + 4) % 4
            qf[2 + it, j * ROWS:(j + 1) * ROWS, :] = qg[it, slot]
        return qf[2 + it, :, 0:NS]

    def exchange_gram(it, gram):
        gg[it, feat] = pack(gram)
        copies = []
        for dx, dy in PLANE:
            r = dx * 4 + dy
            copies.append(send(gg.at[it, feat], gg.at[it, feat], g_s.at[it, r], g_r.at[it, r], (samp, across(dx, dy))))
        return copies

    def join_gram(it, copies):
        for copy in copies:
            copy.wait_recv()
        total = gg[it, 0]
        for j in range(1, 16):
            total = total + gg[it, j]
        return unpack(total)

    q = jnp.zeros((K, NS), F32)
    for p in range(NP):
        dc, sc = d_copies[p]
        sc.wait()
        dc.wait()
        q = q + dot_nt(sv[p], dv[p, 0:NS, :])
    pl.semaphore_wait(barrier, 30)
    copies = reduce_scatter_q(0, jnp.concatenate([q, jnp.zeros((K, K), F32)], axis=1))

    def energy_step(p, total):
        wide = dv[p, 0:NS, :].astype(F32)
        return total + jnp.sum(wide * wide, axis=0, keepdims=True)

    energy = lax.fori_loop(0, NP, energy_step, jnp.zeros((1, PW), F32))
    es[samp] = jnp.broadcast_to(jnp.sum(energy, axis=1, keepdims=True), (8, 128))
    copies = gather_q(0, copies)
    energy_copies = []
    for r in range(1, 16):
        energy_copies.append(send(es.at[samp], es.at[samp], e_s.at[r], e_r.at[r], ((samp + r) % 16, feat)))
    projected = join_q(0, copies).astype(BF16)

    def pull_and_scatter(it, projected):
        pair = {}

        def compute(d):
            there = (z + d) % 8
            psend[it, d] = dot_nn(projected, dv[(1 - c) * 8 + there, 0:NS, :]).astype(BF16)
            pair[d] = send(psend.at[it, d], precv.at[it, d], pair_s.at[it, d], pair_r.at[it, d], sibling)
            acc[d] = dot_nn(projected, dv[c * 8 + there, 0:NS, :])

        def both(d):
            pair[d].wait_recv()
            return acc[d] + precv[it, d].astype(F32)

        def post(slot, value, dev):
            msg_s[it, slot] = value.astype(BF16)
            return send(msg_s.at[it, slot], msg_r.at[it, slot], rs_s.at[it, slot], rs_r.at[it, slot], dev)

        def post_half(slot, value, dev):
            half_s[it, slot] = value.astype(BF16)
            return send(half_s.at[it, slot], half_r.at[it, slot], rs_s.at[it, 6 + slot], rs_r.at[it, 6 + slot], dev)

        compute(4)
        compute(3)
        compute(5)
        compute(2)
        part = both(4)
        far_r = post_half(0, part[:, 0:HALF], chip(2))
        far_l = post_half(1, part[:, HALF:], chip(6))
        mid_r = post(0, both(3), chip(1))
        mid_l = post(1, both(5), chip(7))
        compute(6)
        compute(1)
        compute(7)
        near_r = post(2, both(1), chip(1))
        near_l = post(3, both(7), chip(7))
        compute(0)
        acc[2] = both(2)
        acc[6] = both(6)
        mid_r.wait_recv()
        far_r.wait_recv()
        part = acc[2] + msg_r[it, 0].astype(F32)
        half = half_r[it, 0].astype(F32)
        sum_r = post(4, jnp.concatenate([part[:, 0:HALF] + half, part[:, HALF:]], axis=1), chip(2))
        mid_l.wait_recv()
        far_l.wait_recv()
        part = acc[6] + msg_r[it, 1].astype(F32)
        half = half_r[it, 1].astype(F32)
        sum_l = post(5, jnp.concatenate([part[:, 0:HALF], part[:, HALF:] + half], axis=1), chip(6))
        part = both(0)
        near_r.wait_recv()
        near_l.wait_recv()
        part = part + msg_r[it, 2].astype(F32) + msg_r[it, 3].astype(F32)
        sum_r.wait_recv()
        sum_l.wait_recv()
        return (part + msg_r[it, 4].astype(F32) + msg_r[it, 5].astype(F32)).astype(BF16)

    def gather(it, slot, use):
        here = c * 8
        there = (1 - c) * 8
        sib = {}

        def pass_on(k, d, dev, cols=None):
            p = here + (z + d) % 8
            ref = slot(p) if cols is None else slot(p).at[:, cols]
            return send(ref, ref, ag_s.at[it, k], ag_r.at[it, k], dev)

        def to_sibling(d):
            p = here + (z + d) % 8
            sib[d] = send(slot(p), slot(p), sib_s.at[it, d], sib_r.at[it, d], sibling)

        def use_sibling(d):
            sib[d].wait_recv()
            use(there + (z + d) % 8)

        two_r = pass_on(0, 0, chip(2))
        two_l = pass_on(1, 0, chip(6))
        one_r = pass_on(2, 0, chip(1))
        one_l = pass_on(3, 0, chip(7))
        to_sibling(0)
        use(here + z)
        use_sibling(0)
        one_r.wait_recv()
        to_sibling(7)
        one_l.wait_recv()
        to_sibling(1)
        two_r.wait_recv()
        four_r = pass_on(4, 6, chip(2), slice(0, HALF))
        three_r = pass_on(6, 6, chip(1))
        to_sibling(6)
        two_l.wait_recv()
        four_l = pass_on(5, 2, chip(6), slice(HALF, PW))
        three_l = pass_on(7, 2, chip(7))
        to_sibling(2)
        for d in (7, 1, 6, 2):
            use(here + (z + d) % 8)
        for d in (7, 1, 6, 2):
            use_sibling(d)
        three_r.wait_recv()
        to_sibling(5)
        three_l.wait_recv()
        to_sibling(3)
        use(here + (z + 5) % 8)
        use(here + (z + 3) % 8)
        four_r.wait_recv()
        four_l.wait_recv()
        to_sibling(4)
        use(here + (z + 4) % 8)
        use_sibling(5)
        use_sibling(3)
        use_sibling(4)

    piece = pull_and_scatter(0, projected)
    dv[c * 8 + z, NS:, :] = piece
    qf[0] = jnp.zeros((K, WQ), F32)

    def use_first(p):
        qf[0] += dot_nt(dv[p, NS:, :], dv[p])

    gather(0, lambda p: dv.at[p, NS:, :], use_first)
    copies = reduce_scatter_q(1, qf[0])
    gram_copies = exchange_gram(0, qf[0, :, NS:])
    copies = gather_q(1, copies)
    inv = inverse_factor(join_gram(0, gram_copies))
    projected = dot_exact(inv, join_q(1, copies)).astype(BF16)

    piece = pull_and_scatter(1, projected)
    x2[c * 8 + z] = piece
    qf[1] = jnp.zeros((K, WQ), F32)

    def use_second(p):
        block = x2[p]
        qf[1, :, 0:NS] += dot_nt(block, dv[p, 0:NS, :])
        acc[0, :, 0:K] += dot_nt(block, block)

    acc[0] = jnp.zeros((K, PW), F32)
    gather(1, lambda p: x2.at[p], use_second)
    gram_copies = exchange_gram(1, acc[0, :, 0:K])

    along = qf[1, :, 0:NS]
    cs[...] = pack(lax.dot_general(along, along, (((1,), (1,)), ((), ())), preferred_element_type=F32,
                                   precision=lax.Precision.HIGHEST))
    copy = send(cs, cr, c_s.at[0], c_r.at[0], sibling)
    copy.wait_recv()
    cg[z] = cs[...] + cr[...]
    c_copies = []
    for d in COLUMN:
        c_copies.append(send(cg.at[z], cg.at[z], c_s.at[d], c_r.at[d], chip(d)))
    inv = inverse_factor(join_gram(1, gram_copies))

    scaled = inv * math.sqrt(FEATURES)
    high = scaled.astype(BF16)
    low = (scaled - high.astype(F32)).astype(BF16)
    stacked = jnp.concatenate([high, low], axis=0)
    outs = []
    for p in range(NP):
        two = dot_nn(stacked, x2[p])
        dout[p] = two[0:K] + two[K:]
        oc = pltpu.make_async_copy(dout.at[p], dir_hbm.at[:, p * PW:(p + 1) * PW], o_sem.at[p])
        oc.start()
        outs.append(oc)
    for copy in energy_copies:
        copy.wait_recv()
    energy = es[0]
    for r in range(1, 16):
        energy = energy + es[r]
    for copy in c_copies:
        copy.wait_recv()
    total = cg[0]
    for d in range(1, 8):
        total = total + cg[d]
    spread = dot_exact(inv, unpack(total)) * inv
    captured = lax.dot_general(jnp.ones((8, K), F32), spread, (((1,), (1,)), ((), ())),
                               preferred_element_type=F32, precision=lax.Precision.HIGHEST)
    score_ref[...] = FEATURES * captured[0:1, :] / (energy[0:1, 0:K] + 1e-6)
    for oc in outs:
        oc.wait()
    for copy in pending:
        copy.wait_send()


def on_device(differences, start_block):
    dma = pltpu.SemaphoreType.DMA
    return pl.pallas_call(
        kernel,
        out_shape=(jax.ShapeDtypeStruct((K, WF), F32), jax.ShapeDtypeStruct((1, K), F32)),
        in_specs=[pl.BlockSpec(memory_space=pltpu.HBM), pl.BlockSpec(memory_space=pltpu.HBM)],
        out_specs=(pl.BlockSpec(memory_space=pltpu.HBM), pl.BlockSpec(memory_space=pltpu.VMEM)),
        scratch_shapes=[
            pltpu.VMEM((NP, WQ, PW), BF16),
            pltpu.VMEM((NP, K, PW), BF16),
            pltpu.VMEM((NP, K, PW), BF16),
            pltpu.VMEM((2, 8, K, PW), BF16),
            pltpu.VMEM((2, 8, K, PW), BF16),
            pltpu.VMEM((2, 6, K, PW), BF16),
            pltpu.VMEM((2, 6, K, PW), BF16),
            pltpu.VMEM((2, 2, K, HALF), BF16),
            pltpu.VMEM((2, 2, K, HALF), BF16),
            pltpu.VMEM((8, K, PW), F32),
            pltpu.VMEM((2, 16, ROWS, WQ), F32),
            pltpu.VMEM((2, 16, ROWS, WQ), F32),
            pltpu.VMEM((2, ROWS, WQ), F32),
            pltpu.VMEM((2, 16, ROWS, WQ), F32),
            pltpu.VMEM((4, K, WQ), F32),
            pltpu.VMEM((2, 16, K // 2, 128), F32),
            pltpu.VMEM((16, 8, 128), F32),
            pltpu.VMEM((K // 2, 128), F32),
            pltpu.VMEM((K // 2, 128), F32),
            pltpu.VMEM((8, K // 2, 128), F32),
            pltpu.VMEM((NP, K, PW), F32),
            dma((NP,)), dma((NP,)), dma((NP,)),
            dma((2, 2, 16)), dma((2, 2, 16)),
            dma((2, 8)), dma((2, 8)),
            dma((2, 8)), dma((2, 8)),
            dma((2, 8)), dma((2, 8)),
            dma((2, 8)), dma((2, 8)),
            dma((2, 16)), dma((2, 16)),
            dma((16,)), dma((16,)),
            dma((8,)), dma((8,)),
        ],
        compiler_params=pltpu.CompilerParams(collective_id=0, has_side_effects=True, vmem_limit_bytes=56 * 1024 * 1024),
    )(differences, start_block)


def solution(mesh):
    in_specs = (P("samp", "feat"), P(None, "feat"))
    out_specs = (P(None, "feat"), P("feat", None))
    return jax.shard_map(
        on_device, mesh=mesh, in_specs=in_specs, out_specs=out_specs, check_vma=False
    )
```

time: 635 us -> 98.6 us (0.16)
  blocking collectives: 279 us -> 0 us
  waiting for transfers between devices: 258 us -> 0 us
  Pallas kernels: 0 us -> 94.2 us
  matrix products: 47.2 us -> 0 us
  other arithmetic: 33.8 us -> 0 us
  between operations: 14.8 us -> 0.65 us
    psum x5 -> x0, blocking collectives: 279 us -> none  [the longest x2 121 us: on_device(): gram = lax.psum(local_gram, 'feat')]
    psum x2 -> x0, waiting for transfers between devices: 258 us -> none  [on_device(): pulled = lax.psum(partial_cols, 'samp')]
    pallas_call x0 -> x1, Pallas kernels: none -> 94.2 us  [on_device(): pl.pallas_call(kernel, out_shape=(jax.ShapeDtypeStruct((K, WF), F32), jax...]
    dot_general x7 -> x0, matrix products: 42 us -> none  [the longest x2 13.8 us: on_device(): jnp.dot(projected, differences, preferred_element_type=jnp.float32)]
    another operation x10 -> x0, other arithmetic: 24.1 us -> none  [the longest x6 13 us: orthonormal(): lower = jnp.linalg.cholesky(gram)]
    dot_general x1 -> x0, other arithmetic: 9.15 us -> none  [on_device(): jnp.einsum('sjw,sjw->j', stacked, stacked, preferred_element_type=jnp.flo...]
  transfers between devices with their start and end apart: 2 -> 0, of which waited for: 2 -> 0; matrix products, arithmetic and copies ran while one was open for 1% -> 0% of each run, Pallas kernels for 0% -> 0%
where the time goes in v2:
time: 98.6 us; the launch traced here: 98.5 us
  Pallas kernels  94.2 us (96%)
  local copies, waits for them, and re-layouts  3.58 us (4%)
    pallas_call x1, Pallas kernels, on_device(): pl.pallas_call(kernel, out_shape=(jax.ShapeDtypeStruct((K, WF), F32), jax...  94.2 us
    unnamed x4, local copies, waits for them, and re-layouts  3.58 us

profile of v2, /device:TPU:1, one launch (start us, length us, event | category | flops | bytes accessed | tf_op | source)
XLA Modules:
  0.0 98.5 jit_solution(1884209153442416130)
XLA Ops:
  0.6 94.2 %shard_map.41 = (f32[64,8192]{1,0:T(8,128)}, f32[1,64]{1,0:T(1,128)}) custom-call(bf16[576,8192]{1,0:T(8,128)(2,1)} %d_hbm.1, bf16[64,8192]{1,0:T(8,128)(2,1)} %s_hbm.1), custom_call_target="tpu_custom_call" | custom-call | tf_op jit(solution)/shard_map/pallas_call | solution.py:370
  94.9 0.0 copy-start
  94.9 3.1 %copy.6 = f32[64,8192]{1,0:T(8,128)} copy(f32[64,8192]{1,0:T(8,128)} %get-tuple-element.4) | data formatting | bytes 4194304
  97.9 0.0 copy-done
  97.9 0.5 copy.7
Async XLA Ops:
  94.9 3.1 %copy-start = (f32[1,64]{1,0:T(1,128)S(1)}, f32[1,64]{1,0:T(1,128)}, u32[]{:S(2)}) copy-start(f32[1,64]{1,0:T(1,128)} %get-tuple-element.5) | copy-start | bytes 772

commit v3 on v2

--- a/solution.py
+++ b/solution.py
@@ -13,7 +13,9 @@
 WF = 8192
 NP = 16
 PW = WF // NP
-HALF = PW // 2
+CHUNKS = 2
+CW = PW // CHUNKS
+HALF = CW // 2
 ROWS = K // 16
 WQ = NS + K
 MESH = pl.DeviceIdType.MESH
@@ -77,9 +79,9 @@
 COLUMN = [4, 3, 5, 2, 6, 1, 7]
 
 
-def kernel(d_hbm, s_hbm, dir_hbm, score_ref,
+def kernel(d_hbm, s_hbm, x2_out, factor_ref, score_ref,
            dv, sv, x2, psend, precv, msg_s, msg_r, half_s, half_r, acc,
-           qs, qr, qo, qg, qf, gg, es, cs, cr, cg, dout,
+           qs, qr, qo, qg, qf, gg, es, cs, cr, cg, g2,
            d_sem, s_sem, o_sem, ar_s, ar_r, pair_s, pair_r, rs_s, rs_r,
            ag_s, ag_r, sib_s, sib_r, g_s, g_r, e_s, e_r, c_s, c_r):
     samp = lax.axis_index("samp")
@@ -198,130 +200,151 @@
             pair[d].wait_recv()
             return acc[d] + precv[it, d].astype(F32)
 
-        def post(slot, value, dev):
-            msg_s[it, slot] = value.astype(BF16)
-            return send(msg_s.at[it, slot], msg_r.at[it, slot], rs_s.at[it, slot], rs_r.at[it, slot], dev)
-
-        def post_half(slot, value, dev):
-            half_s[it, slot] = value.astype(BF16)
-            return send(half_s.at[it, slot], half_r.at[it, slot], rs_s.at[it, 6 + slot], rs_r.at[it, 6 + slot], dev)
+        def post(slot, ch, value, dev):
+            msg_s[it, ch, slot] = value.astype(BF16)
+            return send(msg_s.at[it, ch, slot], msg_r.at[it, ch, slot], rs_s.at[it, ch, slot], rs_r.at[it, ch, slot], dev)
+
+        def post_half(slot, ch, value, dev):
+            half_s[it, ch, slot] = value.astype(BF16)
+            return send(half_s.at[it, ch, slot], half_r.at[it, ch, slot],
+                        rs_s.at[it, ch, 6 + slot], rs_r.at[it, ch, 6 + slot], dev)
+
+        def cols(ch):
+            return slice(ch * CW, (ch + 1) * CW)
 
         compute(4)
         compute(3)
         compute(5)
         compute(2)
-        part = both(4)
-        far_r = post_half(0, part[:, 0:HALF], chip(2))
-        far_l = post_half(1, part[:, HALF:], chip(6))
-        mid_r = post(0, both(3), chip(1))
-        mid_l = post(1, both(5), chip(7))
+        part4, part3, part5 = both(4), both(3), both(5)
+        far_r, far_l, mid_r, mid_l, near_r, near_l, sum_r, sum_l = [[None] * CHUNKS for _ in range(8)]
+        for ch in range(CHUNKS):
+            part = part4[:, cols(ch)]
+            far_r[ch] = post_half(0, ch, part[:, 0:HALF], chip(2))
+            far_l[ch] = post_half(1, ch, part[:, HALF:], chip(6))
+            mid_r[ch] = post(0, ch, part3[:, cols(ch)], chip(1))
+            mid_l[ch] = post(1, ch, part5[:, cols(ch)], chip(7))
         compute(6)
         compute(1)
         compute(7)
-        near_r = post(2, both(1), chip(1))
-        near_l = post(3, both(7), chip(7))
+        part1, part7 = both(1), both(7)
+        for ch in range(CHUNKS):
+            near_r[ch] = post(2, ch, part1[:, cols(ch)], chip(1))
+            near_l[ch] = post(3, ch, part7[:, cols(ch)], chip(7))
         compute(0)
         acc[2] = both(2)
         acc[6] = both(6)
-        mid_r.wait_recv()
-        far_r.wait_recv()
-        part = acc[2] + msg_r[it, 0].astype(F32)
-        half = half_r[it, 0].astype(F32)
-        sum_r = post(4, jnp.concatenate([part[:, 0:HALF] + half, part[:, HALF:]], axis=1), chip(2))
-        mid_l.wait_recv()
-        far_l.wait_recv()
-        part = acc[6] + msg_r[it, 1].astype(F32)
-        half = half_r[it, 1].astype(F32)
-        sum_l = post(5, jnp.concatenate([part[:, 0:HALF], part[:, HALF:] + half], axis=1), chip(6))
-        part = both(0)
-        near_r.wait_recv()
-        near_l.wait_recv()
-        part = part + msg_r[it, 2].astype(F32) + msg_r[it, 3].astype(F32)
-        sum_r.wait_recv()
-        sum_l.wait_recv()
-        return (part + msg_r[it, 4].astype(F32) + msg_r[it, 5].astype(F32)).astype(BF16)
-
-    def gather(it, slot, use):
+        for ch in range(CHUNKS):
+            mid_r[ch].wait_recv()
+            far_r[ch].wait_recv()
+            part = acc[2, :, cols(ch)] + msg_r[it, ch, 0].astype(F32)
+            half = half_r[it, ch, 0].astype(F32)
+            sum_r[ch] = post(4, ch, jnp.concatenate([part[:, 0:HALF] + half, part[:, HALF:]], axis=1), chip(2))
+            mid_l[ch].wait_recv()
+            far_l[ch].wait_recv()
+            part = acc[6, :, cols(ch)] + msg_r[it, ch, 1].astype(F32)
+            half = half_r[it, ch, 1].astype(F32)
+            sum_l[ch] = post(5, ch, jnp.concatenate([part[:, 0:HALF], part[:, HALF:] + half], axis=1), chip(6))
+        acc[0] = both(0)
+        for ch in range(CHUNKS):
+            near_r[ch].wait_recv()
+            near_l[ch].wait_recv()
+            part = acc[0, :, cols(ch)] + msg_r[it, ch, 2].astype(F32) + msg_r[it, ch, 3].astype(F32)
+            sum_r[ch].wait_recv()
+            sum_l[ch].wait_recv()
+            yield (part + msg_r[it, ch, 4].astype(F32) + msg_r[it, ch, 5].astype(F32)).astype(BF16)
+
+    def gather(it, slot, pieces, use):
         here = c * 8
         there = (1 - c) * 8
         sib = {}
-
-        def pass_on(k, d, dev, cols=None):
-            p = here + (z + d) % 8
-            ref = slot(p) if cols is None else slot(p).at[:, cols]
-            return send(ref, ref, ag_s.at[it, k], ag_r.at[it, k], dev)
-
-        def to_sibling(d):
-            p = here + (z + d) % 8
-            sib[d] = send(slot(p), slot(p), sib_s.at[it, d], sib_r.at[it, d], sibling)
-
-        def use_sibling(d):
-            sib[d].wait_recv()
-            use(there + (z + d) % 8)
-
-        two_r = pass_on(0, 0, chip(2))
-        two_l = pass_on(1, 0, chip(6))
-        one_r = pass_on(2, 0, chip(1))
-        one_l = pass_on(3, 0, chip(7))
-        to_sibling(0)
-        use(here + z)
-        use_sibling(0)
-        one_r.wait_recv()
-        to_sibling(7)
-        one_l.wait_recv()
-        to_sibling(1)
-        two_r.wait_recv()
-        four_r = pass_on(4, 6, chip(2), slice(0, HALF))
-        three_r = pass_on(6, 6, chip(1))
-        to_sibling(6)
-        two_l.wait_recv()
-        four_l = pass_on(5, 2, chip(6), slice(HALF, PW))
-        three_l = pass_on(7, 2, chip(7))
-        to_sibling(2)
-        for d in (7, 1, 6, 2):
-            use(here + (z + d) % 8)
-        for d in (7, 1, 6, 2):
-            use_sibling(d)
-        three_r.wait_recv()
-        to_sibling(5)
-        three_l.wait_recv()
-        to_sibling(3)
-        use(here + (z + 5) % 8)
-        use(here + (z + 3) % 8)
-        four_r.wait_recv()
-        four_l.wait_recv()
-        to_sibling(4)
-        use(here + (z + 4) % 8)
-        use_sibling(5)
-        use_sibling(3)
-        use_sibling(4)
-
-    piece = pull_and_scatter(0, projected)
-    dv[c * 8 + z, NS:, :] = piece
+        two_r, two_l, one_r, one_l, four_r, four_l, three_r, three_l = [[None] * CHUNKS for _ in range(8)]
+
+        def pass_on(k, ch, d, dev, start=0, width=CW):
+            ref = slot(here + (z + d) % 8, slice(ch * CW + start, ch * CW + start + width))
+            return send(ref, ref, ag_s.at[it, ch, k], ag_r.at[it, ch, k], dev)
+
+        def to_sibling(ch, d):
+            ref = slot(here + (z + d) % 8, slice(ch * CW, (ch + 1) * CW))
+            sib[ch, d] = send(ref, ref, sib_s.at[it, ch, d], sib_r.at[it, ch, d], sibling)
+
+        def use_own(ch, d):
+            use(here + (z + d) % 8, slice(ch * CW, (ch + 1) * CW))
+
+        def use_sibling(ch, d):
+            sib[ch, d].wait_recv()
+            use(there + (z + d) % 8, slice(ch * CW, (ch + 1) * CW))
+
+        for ch, piece in enumerate(pieces):
+            slot(here + z, slice(ch * CW, (ch + 1) * CW))[...] = piece
+            two_r[ch] = pass_on(0, ch, 0, chip(2))
+            two_l[ch] = pass_on(1, ch, 0, chip(6))
+            one_r[ch] = pass_on(2, ch, 0, chip(1))
+            one_l[ch] = pass_on(3, ch, 0, chip(7))
+            to_sibling(ch, 0)
+        for ch in range(CHUNKS):
+            use_own(ch, 0)
+        for ch in range(CHUNKS):
+            use_sibling(ch, 0)
+        for ch in range(CHUNKS):
+            one_r[ch].wait_recv()
+            to_sibling(ch, 7)
+            one_l[ch].wait_recv()
+            to_sibling(ch, 1)
+            two_r[ch].wait_recv()
+            four_r[ch] = pass_on(4, ch, 6, chip(2), 0, HALF)
+            three_r[ch] = pass_on(6, ch, 6, chip(1))
+            to_sibling(ch, 6)
+            two_l[ch].wait_recv()
+            four_l[ch] = pass_on(5, ch, 2, chip(6), HALF, HALF)
+            three_l[ch] = pass_on(7, ch, 2, chip(7))
+            to_sibling(ch, 2)
+            for d in (7, 1):
+                use_own(ch, d)
+        for ch in range(CHUNKS):
+            for d in (6, 2):
+                use_own(ch, d)
+            for d in (7, 1, 6, 2):
+                use_sibling(ch, d)
+        for ch in range(CHUNKS):
+            three_r[ch].wait_recv()
+            to_sibling(ch, 5)
+            three_l[ch].wait_recv()
+            to_sibling(ch, 3)
+            four_r[ch].wait_recv()
+            four_l[ch].wait_recv()
+            to_sibling(ch, 4)
+            for d in (5, 3, 4):
+                use_own(ch, d)
+        for ch in range(CHUNKS):
+            for d in (5, 3, 4):
+                use_sibling(ch, d)
+
     qf[0] = jnp.zeros((K, WQ), F32)
 
-    def use_first(p):
-        qf[0] += dot_nt(dv[p, NS:, :], dv[p])
-
-    gather(0, lambda p: dv.at[p, NS:, :], use_first)
+    def use_first(p, cols):
+        qf[0] += dot_nt(dv[p, NS:, cols], dv[p, :, cols])
+
+    gather(0, lambda p, cols: dv.at[p, NS:, cols], pull_and_scatter(0, projected), use_first)
     copies = reduce_scatter_q(1, qf[0])
     gram_copies = exchange_gram(0, qf[0, :, NS:])
     copies = gather_q(1, copies)
     inv = inverse_factor(join_gram(0, gram_copies))
     projected = dot_exact(inv, join_q(1, copies)).astype(BF16)
 
-    piece = pull_and_scatter(1, projected)
-    x2[c * 8 + z] = piece
     qf[1] = jnp.zeros((K, WQ), F32)
 
-    def use_second(p):
-        block = x2[p]
-        qf[1, :, 0:NS] += dot_nt(block, dv[p, 0:NS, :])
-        acc[0, :, 0:K] += dot_nt(block, block)
-
-    acc[0] = jnp.zeros((K, PW), F32)
-    gather(1, lambda p: x2.at[p], use_second)
-    gram_copies = exchange_gram(1, acc[0, :, 0:K])
+    g2[...] = jnp.zeros((K, K), F32)
+
+    def use_second(p, cols):
+        block = x2[p, :, cols]
+        qf[1, :, 0:NS] += dot_nt(block, dv[p, 0:NS, cols])
+        g2[...] += dot_nt(block, block)
+
+    gather(1, lambda p, cols: x2.at[p, :, cols], pull_and_scatter(1, projected), use_second)
+    gram_copies = exchange_gram(1, g2[...])
+    out_copy = pltpu.make_async_copy(x2, x2_out, o_sem)
+    out_copy.start()
 
     along = qf[1, :, 0:NS]
     cs[...] = pack(lax.dot_general(along, along, (((1,), (1,)), ((), ())), preferred_element_type=F32,
@@ -337,14 +360,7 @@
     scaled = inv * math.sqrt(FEATURES)
     high = scaled.astype(BF16)
     low = (scaled - high.astype(F32)).astype(BF16)
-    stacked = jnp.concatenate([high, low], axis=0)
-    outs = []
-    for p in range(NP):
-        two = dot_nn(stacked, x2[p])
-        dout[p] = two[0:K] + two[K:]
-        oc = pltpu.make_async_copy(dout.at[p], dir_hbm.at[:, p * PW:(p + 1) * PW], o_sem.at[p])
-        oc.start()
-        outs.append(oc)
+    factor_ref[...] = jnp.concatenate([high, low], axis=0)
     for copy in energy_copies:
         copy.wait_recv()
     energy = es[0]
@@ -359,29 +375,37 @@
     captured = lax.dot_general(jnp.ones((8, K), F32), spread, (((1,), (1,)), ((), ())),
                                preferred_element_type=F32, precision=lax.Precision.HIGHEST)
     score_ref[...] = FEATURES * captured[0:1, :] / (energy[0:1, 0:K] + 1e-6)
-    for oc in outs:
-        oc.wait()
+    out_copy.wait()
     for copy in pending:
         copy.wait_send()
 
 
+def write_directions(pulled_ref, factor_ref, score_in, dir_ref, score_ref):
+    score_ref[...] = score_in[...]
+    for i in range(pulled_ref.shape[0]):
+        two = dot_nn(factor_ref[...], pulled_ref[i])
+        dir_ref[:, i * PW:(i + 1) * PW] = two[0:K] + two[K:]
+
+
 def on_device(differences, start_block):
     dma = pltpu.SemaphoreType.DMA
-    return pl.pallas_call(
+    pulled, factor, scores = pl.pallas_call(
         kernel,
-        out_shape=(jax.ShapeDtypeStruct((K, WF), F32), jax.ShapeDtypeStruct((1, K), F32)),
+        out_shape=(jax.ShapeDtypeStruct((NP, K, PW), BF16), jax.ShapeDtypeStruct((2 * K, K), BF16),
+                   jax.ShapeDtypeStruct((1, K), F32)),
         in_specs=[pl.BlockSpec(memory_space=pltpu.HBM), pl.BlockSpec(memory_space=pltpu.HBM)],
-        out_specs=(pl.BlockSpec(memory_space=pltpu.HBM), pl.BlockSpec(memory_space=pltpu.VMEM)),
+        out_specs=(pl.BlockSpec(memory_space=pltpu.HBM), pl.BlockSpec(memory_space=pltpu.VMEM),
+                   pl.BlockSpec(memory_space=pltpu.VMEM)),
         scratch_shapes=[
             pltpu.VMEM((NP, WQ, PW), BF16),
             pltpu.VMEM((NP, K, PW), BF16),
             pltpu.VMEM((NP, K, PW), BF16),
             pltpu.VMEM((2, 8, K, PW), BF16),
             pltpu.VMEM((2, 8, K, PW), BF16),
-            pltpu.VMEM((2, 6, K, PW), BF16),
-            pltpu.VMEM((2, 6, K, PW), BF16),
-            pltpu.VMEM((2, 2, K, HALF), BF16),
-            pltpu.VMEM((2, 2, K, HALF), BF16),
+            pltpu.VMEM((2, CHUNKS, 6, K, CW), BF16),
+            pltpu.VMEM((2, CHUNKS, 6, K, CW), BF16),
+            pltpu.VMEM((2, CHUNKS, 2, K, HALF), BF16),
+            pltpu.VMEM((2, CHUNKS, 2, K, HALF), BF16),
             pltpu.VMEM((8, K, PW), F32),
             pltpu.VMEM((2, 16, ROWS, WQ), F32),
             pltpu.VMEM((2, 16, ROWS, WQ), F32),
@@ -393,19 +417,28 @@
             pltpu.VMEM((K // 2, 128), F32),
             pltpu.VMEM((K // 2, 128), F32),
             pltpu.VMEM((8, K // 2, 128), F32),
-            pltpu.VMEM((NP, K, PW), F32),
-            dma((NP,)), dma((NP,)), dma((NP,)),
+            pltpu.VMEM((K, K), F32),
+            dma((NP,)), dma((NP,)), dma,
             dma((2, 2, 16)), dma((2, 2, 16)),
             dma((2, 8)), dma((2, 8)),
-            dma((2, 8)), dma((2, 8)),
-            dma((2, 8)), dma((2, 8)),
-            dma((2, 8)), dma((2, 8)),
+            dma((2, CHUNKS, 8)), dma((2, CHUNKS, 8)),
+            dma((2, CHUNKS, 8)), dma((2, CHUNKS, 8)),
+            dma((2, CHUNKS, 8)), dma((2, CHUNKS, 8)),
             dma((2, 16)), dma((2, 16)),
             dma((16,)), dma((16,)),
             dma((8,)), dma((8,)),
         ],
         compiler_params=pltpu.CompilerParams(collective_id=0, has_side_effects=True, vmem_limit_bytes=56 * 1024 * 1024),
     )(differences, start_block)
+    step = 4
+    return pl.pallas_call(
+        write_directions,
+        grid=(NP // step,),
+        out_shape=(jax.ShapeDtypeStruct((K, WF), F32), jax.ShapeDtypeStruct((1, K), F32)),
+        in_specs=[pl.BlockSpec((step, K, PW), lambda i: (i, 0, 0)), pl.BlockSpec((2 * K, K), lambda i: (0, 0)),
+                  pl.BlockSpec((1, K), lambda i: (0, 0))],
+        out_specs=(pl.BlockSpec((K, step * PW), lambda i: (0, i)), pl.BlockSpec((1, K), lambda i: (0, 0))),
+    )(pulled, factor, scores)
 
 
 def solution(mesh):

time: 98.6 us -> 98.2 us (level)
  local copies, waits for them, and re-layouts: 3.58 us -> 0 us
  Pallas kernels: 94.2 us -> 97.4 us
    unnamed x4 -> x0, local copies, waits for them, and re-layouts: 3.58 us -> none
    pallas_call x1 -> x2, Pallas kernels: 94.2 us -> 97.4 us  [the longest x1 93.3 us: on_device(): pl.pallas_call(kernel, out_shape=(jax.ShapeDtypeStruct((NP, K, PW), BF16)...]
where the time goes in v3:
time: 98.2 us; the launch traced here: 98 us
  Pallas kernels  97.4 us (99%)
    pallas_call x1, Pallas kernels, on_device(): pl.pallas_call(kernel, out_shape=(jax.ShapeDtypeStruct((NP, K, PW), BF16)...  93.3 us
    pallas_call x1, Pallas kernels, on_device(): pl.pallas_call(write_directions, grid=(NP // step,), out_shape=(jax.Shape...  4.07 us

profile of v3, /device:TPU:1, one launch (start us, length us, event | category | flops | bytes accessed | tf_op | source)
XLA Modules:
  0.0 98.0 jit_solution(9767965056381392803)
XLA Ops:
  0.6 93.3 %shard_map.41 = (bf16[16,64,512]{2,1,0:T(8,128)(2,1)}, bf16[128,64]{1,0:T(8,128)(2,1)}, f32[1,64]{1,0:T(1,128)}) custom-call(bf16[576,8192]{1,0:T(8,128)(2,1)} %d_hbm.1, bf16[64,8192]{1,0:T(8,128)(2,1)} %s_hbm.1), custom_call_target="tpu_custom_call" | custom-call | tf_op jit(solution)/shard_map/pallas_call | solution.py:392
  94.0 4.1 %shard_map.42 = (f32[64,8192]{1,0:T(8,128)}, f32[1,64]{1,0:T(1,128)}) custom-call(bf16[16,64,512]{2,1,0:T(8,128)(2,1)} %get-tuple-element.5.pulled_ref, bf16[128,64]{1,0:T(8,128)(2,1)} %get-tuple-element.6.factor_ref, f32[1,64]{1,0:T(1,128)} %get-tuple-element.7.score_in), custom_call_target="tpu_custom_call" | custom-call | tf_op jit(solution)/shard_map/pallas_call | solution.py:434

commit v4 on v3

--- a/solution.py
+++ b/solution.py
@@ -18,6 +18,7 @@
 HALF = CW // 2
 ROWS = K // 16
 WQ = NS + K
+GROUPS = 8
 MESH = pl.DeviceIdType.MESH
 F32 = jnp.float32
 BF16 = jnp.bfloat16
@@ -106,6 +107,10 @@
         pending.append(copy)
         return copy
 
+    def flush(keep=0):
+        while len(pending) > keep:
+            pending.pop(0).wait_send()
+
     barrier = pltpu.get_barrier_semaphore()
     for r in range(1, 16):
         pl.semaphore_signal(barrier, inc=1, device_id=(samp, (feat + r) % 16), device_id_type=MESH)
@@ -140,6 +145,7 @@
         for dx, dy in PLANE:
             r = dx * 4 + dy
             copies.append(send(qo.at[it], qg.at[it, r], ar_s.at[it, 1, r], ar_r.at[it, 1, r], (samp, across(dx, dy))))
+        flush(15)
         return copies
 
     def join_q(it, copies):
@@ -268,29 +274,28 @@
             ref = slot(here + (z + d) % 8, slice(ch * CW, (ch + 1) * CW))
             sib[ch, d] = send(ref, ref, sib_s.at[it, ch, d], sib_r.at[it, ch, d], sibling)
 
-        def use_own(ch, d):
-            use(here + (z + d) % 8, slice(ch * CW, (ch + 1) * CW))
-
-        def use_sibling(ch, d):
-            sib[ch, d].wait_recv()
-            use(there + (z + d) % 8, slice(ch * CW, (ch + 1) * CW))
+        def use_own(ch, *ds):
+            use([here + (z + d) % 8 for d in ds], slice(ch * CW, (ch + 1) * CW))
+
+        def use_sibling(ch, *ds):
+            for d in ds:
+                sib[ch, d].wait_recv()
+            use([there + (z + d) % 8 for d in ds], slice(ch * CW, (ch + 1) * CW))
 
         for ch, piece in enumerate(pieces):
             slot(here + z, slice(ch * CW, (ch + 1) * CW))[...] = piece
             two_r[ch] = pass_on(0, ch, 0, chip(2))
             two_l[ch] = pass_on(1, ch, 0, chip(6))
+            to_sibling(ch, 0)
+        for ch in range(CHUNKS):
             one_r[ch] = pass_on(2, ch, 0, chip(1))
             one_l[ch] = pass_on(3, ch, 0, chip(7))
-            to_sibling(ch, 0)
-        for ch in range(CHUNKS):
-            use_own(ch, 0)
-        for ch in range(CHUNKS):
-            use_sibling(ch, 0)
-        for ch in range(CHUNKS):
-            one_r[ch].wait_recv()
-            to_sibling(ch, 7)
-            one_l[ch].wait_recv()
-            to_sibling(ch, 1)
+        use_own(0, 0)
+        use_own(1, 0)
+        use_sibling(0, 0)
+        use_sibling(1, 0)
+        flush(10)
+        for ch in range(CHUNKS):
             two_r[ch].wait_recv()
             four_r[ch] = pass_on(4, ch, 6, chip(2), 0, HALF)
             three_r[ch] = pass_on(6, ch, 6, chip(1))
@@ -299,13 +304,16 @@
             four_l[ch] = pass_on(5, ch, 2, chip(6), HALF, HALF)
             three_l[ch] = pass_on(7, ch, 2, chip(7))
             to_sibling(ch, 2)
-            for d in (7, 1):
-                use_own(ch, d)
-        for ch in range(CHUNKS):
-            for d in (6, 2):
-                use_own(ch, d)
-            for d in (7, 1, 6, 2):
-                use_sibling(ch, d)
+            use_own(ch, 6, 2)
+        for ch in range(CHUNKS):
+            one_r[ch].wait_recv()
+            to_sibling(ch, 7)
+            one_l[ch].wait_recv()
+            to_sibling(ch, 1)
+            use_own(ch, 7, 1)
+            use_sibling(ch, 6, 2)
+        use_sibling(0, 7, 1)
+        use_sibling(1, 7, 1)
         for ch in range(CHUNKS):
             three_r[ch].wait_recv()
             to_sibling(ch, 5)
@@ -314,16 +322,14 @@
             four_r[ch].wait_recv()
             four_l[ch].wait_recv()
             to_sibling(ch, 4)
-            for d in (5, 3, 4):
-                use_own(ch, d)
-        for ch in range(CHUNKS):
-            for d in (5, 3, 4):
-                use_sibling(ch, d)
+            use_own(ch, 5, 3, 4)
+        for ch in range(CHUNKS):
+            use_sibling(ch, 5, 3, 4)
 
     qf[0] = jnp.zeros((K, WQ), F32)
 
-    def use_first(p, cols):
-        qf[0] += dot_nt(dv[p, NS:, cols], dv[p, :, cols])
+    def use_first(ps, cols):
+        qf[0] += sum(dot_nt(dv[p, NS:, cols], dv[p, :, cols]) for p in ps)
 
     gather(0, lambda p, cols: dv.at[p, NS:, cols], pull_and_scatter(0, projected), use_first)
     copies = reduce_scatter_q(1, qf[0])
@@ -336,10 +342,9 @@
 
     g2[...] = jnp.zeros((K, K), F32)
 
-    def use_second(p, cols):
-        block = x2[p, :, cols]
-        qf[1, :, 0:NS] += dot_nt(block, dv[p, 0:NS, cols])
-        g2[...] += dot_nt(block, block)
+    def use_second(ps, cols):
+        qf[1, :, 0:NS] += sum(dot_nt(x2[p, :, cols], dv[p, 0:NS, cols]) for p in ps)
+        g2[...] += sum(dot_nt(x2[p, :, cols], x2[p, :, cols]) for p in ps)
 
     gather(1, lambda p, cols: x2.at[p, :, cols], pull_and_scatter(1, projected), use_second)
     gram_copies = exchange_gram(1, g2[...])
@@ -355,6 +360,7 @@
     c_copies = []
     for d in COLUMN:
         c_copies.append(send(cg.at[z], cg.at[z], c_s.at[d], c_r.at[d], chip(d)))
+    flush(7)
     inv = inverse_factor(join_gram(1, gram_copies))
 
     scaled = inv * math.sqrt(FEATURES)
@@ -376,15 +382,27 @@
                                preferred_element_type=F32, precision=lax.Precision.HIGHEST)
     score_ref[...] = FEATURES * captured[0:1, :] / (energy[0:1, 0:K] + 1e-6)
     out_copy.wait()
-    for copy in pending:
-        copy.wait_send()
-
-
-def write_directions(pulled_ref, factor_ref, score_in, dir_ref, score_ref):
+    flush()
+
+
+def write_directions(pulled_ref, factor_ref, score_in, dir_ref, score_ref, here, out, in_sem, out_sem):
+    reads = []
+    for g in range(GROUPS):
+        part = pl.ds(g * (NP // GROUPS), NP // GROUPS)
+        reads.append(pltpu.make_async_copy(pulled_ref.at[part], here.at[part], in_sem.at[g]))
+        reads[g].start()
     score_ref[...] = score_in[...]
-    for i in range(pulled_ref.shape[0]):
-        two = dot_nn(factor_ref[...], pulled_ref[i])
-        dir_ref[:, i * PW:(i + 1) * PW] = two[0:K] + two[K:]
+    writes = []
+    for g in range(GROUPS):
+        reads[g].wait()
+        for p in range(g * (NP // GROUPS), (g + 1) * (NP // GROUPS)):
+            two = dot_nn(factor_ref[...], here[p])
+            out[:, p * PW:(p + 1) * PW] = two[0:K] + two[K:]
+        cols = pl.ds(g * (WF // GROUPS), WF // GROUPS)
+        writes.append(pltpu.make_async_copy(out.at[:, cols], dir_ref.at[:, cols], out_sem.at[g]))
+        writes[g].start()
+    for copy in writes:
+        copy.wait()
 
 
 def on_device(differences, start_block):
@@ -430,14 +448,13 @@
         ],
         compiler_params=pltpu.CompilerParams(collective_id=0, has_side_effects=True, vmem_limit_bytes=56 * 1024 * 1024),
     )(differences, start_block)
-    step = 4
     return pl.pallas_call(
         write_directions,
-        grid=(NP // step,),
         out_shape=(jax.ShapeDtypeStruct((K, WF), F32), jax.ShapeDtypeStruct((1, K), F32)),
-        in_specs=[pl.BlockSpec((step, K, PW), lambda i: (i, 0, 0)), pl.BlockSpec((2 * K, K), lambda i: (0, 0)),
-                  pl.BlockSpec((1, K), lambda i: (0, 0))],
-        out_specs=(pl.BlockSpec((K, step * PW), lambda i: (0, i)), pl.BlockSpec((1, K), lambda i: (0, 0))),
+        in_specs=[pl.BlockSpec(memory_space=pl.ANY), pl.BlockSpec(memory_space=pltpu.VMEM),
+                  pl.BlockSpec(memory_space=pltpu.VMEM)],
+        out_specs=(pl.BlockSpec(memory_space=pltpu.HBM), pl.BlockSpec(memory_space=pltpu.VMEM)),
+        scratch_shapes=[pltpu.VMEM((NP, K, PW), BF16), pltpu.VMEM((K, WF), F32), dma((GROUPS,)), dma((GROUPS,))],
     )(pulled, factor, scores)
 
 

time: 98.2 us -> 95.9 us (0.977)
  Pallas kernels: 97.4 us -> 94.9 us
    pallas_call x1, Pallas kernels: 93.3 us -> 90.2 us  [on_device(): pl.pallas_call(kernel, out_shape=(jax.ShapeDtypeStruct((NP, K, PW), BF16)...]
where the time goes in v4:
time: 95.9 us; the launch traced here: 95.7 us
  Pallas kernels  94.9 us (99%)
    pallas_call x1, Pallas kernels, on_device(): pl.pallas_call(kernel, out_shape=(jax.ShapeDtypeStruct((NP, K, PW), BF16)...  90.2 us
    pallas_call x1, Pallas kernels, on_device(): pl.pallas_call(write_directions, out_shape=(jax.ShapeDtypeStruct((K, WF),...  4.66 us

profile of v4, /device:TPU:1, one launch (start us, length us, event | category | flops | bytes accessed | tf_op | source)
XLA Modules:
  0.0 95.7 jit_solution(17426840688046482014)
XLA Ops:
  0.6 90.2 %shard_map.41 = (bf16[16,64,512]{2,1,0:T(8,128)(2,1)}, bf16[128,64]{1,0:T(8,128)(2,1)}, f32[1,64]{1,0:T(1,128)}) custom-call(bf16[576,8192]{1,0:T(8,128)(2,1)} %d_hbm.1, bf16[64,8192]{1,0:T(8,128)(2,1)} %s_hbm.1), custom_call_target="tpu_custom_call" | custom-call | tf_op jit(solution)/shard_map/pallas_call | solution.py:410
  90.9 4.7 %shard_map.42 = (f32[64,8192]{1,0:T(8,128)}, f32[1,64]{1,0:T(1,128)}) custom-call(bf16[16,64,512]{2,1,0:T(8,128)(2,1)} %get-tuple-element.5.pulled_ref, bf16[128,64]{1,0:T(8,128)(2,1)} %get-tuple-element.6.factor_ref, f32[1,64]{1,0:T(1,128)} %get-tuple-element.7.score_in), custom_call_target="tpu_custom_call" | custom-call | tf_op jit(solution)/shard_map/pallas_call | solution.py:451

commit v5 on v4

v5 whole, which is shorter than its diff:
```python
import math

import jax
import jax.numpy as jnp
from jax import lax
from jax.experimental import pallas as pl
from jax.experimental.pallas import tpu as pltpu
from jax.sharding import PartitionSpec as P

FEATURES = 131072
K = 64
NS = 576
WF = 8192
NP = 16
PW = WF // NP
CHUNKS = 2
CW = PW // CHUNKS
HALF = CW // 2
ROWS = K // 16
WQ = NS + K
LOAD = 4
MESH = pl.DeviceIdType.MESH
F32 = jnp.float32
BF16 = jnp.bfloat16


def dot_nn(a, b):
    return lax.dot_general(a, b, (((1,), (0,)), ((), ())), preferred_element_type=F32)


def dot_nt(a, b):
    return lax.dot_general(a, b, (((1,), (1,)), ((), ())), preferred_element_type=F32)


def dot_exact(a, b):
    return lax.dot_general(a, b, (((1,), (0,)), ((), ())), preferred_element_type=F32, precision=lax.Precision.HIGHEST)


def inverse_factor(gram):
    row = lax.broadcasted_iota(jnp.int32, (8, 2 * K), 0)
    col = lax.broadcasted_iota(jnp.int32, (8, 2 * K), 1)
    wide = jnp.concatenate([gram, jnp.zeros((K, K), F32)], axis=1)
    m = [wide[8 * g:8 * g + 8, :] + jnp.where(col == row + (K + 8 * g), 1.0, 0.0) for g in range(8)]
    out = []
    for b in range(8):
        cols = [[jnp.broadcast_to(m[g][:, 8 * b + k:8 * b + k + 1], (8, 2 * K)) for k in range(8)] for g in range(b, 8)]
        diag = jnp.zeros((8, 2 * K), F32)
        for k in range(8):
            d = cols[0][k][k:k + 1, :]
            r = 1.0 / d
            diag = jnp.where(row == k, d, diag)
            pivot_row = m[b][k:k + 1, :] * r
            factor = [jnp.where(row > k, cols[0][k], 0.0)] + [cols[i][k] for i in range(1, 8 - b)]
            for i in range(8 - b):
                m[b + i] = m[b + i] - factor[i] * pivot_row
            for kk in range(k + 1, 8):
                t = cols[0][k][kk:kk + 1, :] * r
                for i in range(8 - b):
                    cols[i][kk] = cols[i][kk] - factor[i] * t
        inv = lax.rsqrt(diag)
        inv = inv * (1.5 - 0.5 * ((diag * inv) * inv))
        out.append((m[b] * inv)[:, K:])
    return jnp.concatenate(out, axis=0)


def pack(square):
    return jnp.concatenate([square[0:K // 2], square[K // 2:]], axis=1)


def unpack(wide):
    return jnp.concatenate([wide[:, 0:K], wide[:, K:]], axis=0)


def ring_hops(d, n):
    return min(d, n - d)


PLANE = sorted([(dx, dy) for dx in range(4) for dy in range(4) if dx or dy],
               key=lambda o: -(ring_hops(o[0], 4) + ring_hops(o[1], 4)))
COLUMN = [4, 3, 5, 2, 6, 1, 7]


PAIRS = [4, 3, 5, 1, 7, 2, 6, 0]


def kernel(d_hbm, s_hbm, x2_out, factor_ref, score_ref,
           dv, sv, x2, psend, precv, msg_s, msg_r, half_s, half_r, acc,
           qs, qr, qo, qg, qf, gg, cs, cr, cg, g2,
           d_sem, s_sem, o_sem, ar_s, ar_r, pair_s, pair_r, rs_s, rs_r,
           ag_s, ag_r, sib_s, sib_r, g_s, g_r, c_s, c_r):
    samp = lax.axis_index("samp")
    feat = lax.axis_index("feat")
    z = samp // 2
    c = samp % 2
    x = feat // 4
    y = feat % 4
    sibling = (z * 2 + (1 - c), feat)

    def chip(d):
        return (((z + d) % 8) * 2 + c, feat)

    def across(dx, dy):
        return ((x + dx) % 4) * 4 + (y + dy) % 4

    def send(src, dst, ssem, rsem, dev):
        pltpu.make_async_remote_copy(src_ref=src, dst_ref=dst, send_sem=ssem, recv_sem=rsem,
                                     device_id=dev, device_id_type=MESH).start()

    def wait(ref, sem):
        pltpu.make_async_copy(ref, ref, sem).wait()

    for p in range(NP):
        pltpu.make_async_copy(s_hbm.at[:, p * PW:(p + 1) * PW], sv.at[p], s_sem).start()
    for p in range(NP):
        pltpu.make_async_copy(d_hbm.at[:, p * PW:(p + 1) * PW], dv.at[p, 0:NS, :], d_sem.at[p // LOAD]).start()

    barrier = pltpu.get_barrier_semaphore()
    for dx, dy in PLANE:
        pl.semaphore_signal(barrier, inc=1, device_id=(samp, across(dx, dy)), device_id_type=MESH)
    for d in COLUMN:
        pl.semaphore_signal(barrier, inc=1, device_id=chip(d), device_id_type=MESH)
    pl.semaphore_signal(barrier, inc=1, device_id=sibling, device_id_type=MESH)

    def reduce_scatter_q(it, value):
        for j in range(16):
            qs[it, j] = value[j * ROWS:(j + 1) * ROWS, :]
        for dx, dy in PLANE:
            there = across(dx, dy)
            send(qs.at[it, there], qr.at[it, dx * 4 + dy], ar_s.at[it, 0], ar_r.at[it, 0], (samp, there))

    def gather_q(it):
        total = qs[it, feat]
        wait(qr.at[it, 1:16], ar_r.at[it, 0])
        for r in range(1, 16):
            total = total + qr[it, r]
        qo[it] = total
        qg[it, 0] = total
        for dx, dy in PLANE:
            send(qo.at[it], qg.at[it, dx * 4 + dy], ar_s.at[it, 1], ar_r.at[it, 1], (samp, across(dx, dy)))
        wait(qs.at[it, 1:16], ar_s.at[it, 0])

    def join_q(it):
        wait(qg.at[it, 1:16], ar_r.at[it, 1])
        for j in range(16):
            slot = ((x - j // 4 + 4) % 4) * 4 + (y - j % 4 + 4) % 4
            qf[2 + it, j * ROWS:(j + 1) * ROWS, :] = qg[it, slot]
        return qf[2 + it, :, 0:NS]

    def exchange_gram(it, gram):
        gg[it, 0] = pack(gram)
        for dx, dy in PLANE:
            send(gg.at[it, 0], gg.at[it, dx * 4 + dy], g_s.at[it], g_r.at[it], (samp, across(dx, dy)))

    def join_gram(it):
        wait(gg.at[it, 1:16], g_r.at[it])
        total = gg[it, 0]
        for j in range(1, 16):
            total = total + gg[it, j]
        return unpack(total)

    q = jnp.zeros((K, NS), F32)
    wait(sv, s_sem)
    for p in range(NP):
        if p % LOAD == 0:
            wait(dv.at[p:p + LOAD, 0:NS, :], d_sem.at[p // LOAD])
        q = q + dot_nt(sv[p], dv[p, 0:NS, :])
    pl.semaphore_wait(barrier, 23)
    reduce_scatter_q(0, jnp.concatenate([q, jnp.zeros((K, K), F32)], axis=1))

    def energy_step(p, total):
        wide = dv[p, 0:NS, :].astype(F32)
        return total + jnp.sum(wide * wide, axis=0, keepdims=True)

    energy = lax.fori_loop(0, NP, energy_step, jnp.zeros((1, PW), F32))
    cs[K // 2:, :] = jnp.broadcast_to(jnp.sum(energy, axis=1, keepdims=True), (8, 128))
    gather_q(0)
    projected = join_q(0).astype(BF16)

    def pull_and_scatter(it, projected):
        def compute(d):
            there = (z + d) % 8
            k = PAIRS.index(d)
            psend[it, k] = dot_nn(projected, dv[(1 - c) * 8 + there, 0:NS, :]).astype(BF16)
            group = 0 if k < 3 else 1 if k < 5 else 2 if k < 7 else 3
            send(psend.at[it, k], precv.at[it, k], pair_s.at[it], pair_r.at[it, group], sibling)
            acc[d] = dot_nn(projected, dv[c * 8 + there, 0:NS, :])

        def join(group):
            first, last = ((0, 3), (3, 5), (5, 7), (7, 8))[group]
            wait(precv.at[it, first:last], pair_r.at[it, group])

        def both(d):
            return acc[d] + precv[it, PAIRS.index(d)].astype(F32)

        def post(slot, ch, value, dev):
            msg_s[it, ch, slot] = value.astype(BF16)
            send(msg_s.at[it, ch, slot], msg_r.at[it, ch, slot], rs_s.at[it, 0], rs_r.at[it, ch, slot], dev)

        def post_half(slot, ch, value, dev):
            half_s[it, ch, slot] = value.astype(BF16)
            send(half_s.at[it, ch, slot], half_r.at[it, ch, slot], rs_s.at[it, 1], rs_r.at[it, ch, 6 + slot], dev)

        def arrived(slot, ch):
            wait(msg_r.at[it, ch, slot] if slot < 6 else half_r.at[it, ch, slot - 6], rs_r.at[it, ch, slot])

        def cols(ch):
            return slice(ch * CW, (ch + 1) * CW)

        compute(4)
        compute(3)
        compute(5)
        compute(2)
        join(0)
        part4, part3, part5 = both(4), both(3), both(5)
        for ch in range(CHUNKS):
            part = part4[:, cols(ch)]
            post_half(0, ch, part[:, 0:HALF], chip(2))
            post_half(1, ch, part[:, HALF:], chip(6))
            post(0, ch, part3[:, cols(ch)], chip(1))
            post(1, ch, part5[:, cols(ch)], chip(7))
        compute(6)
        compute(1)
        compute(7)
        join(1)
        part1, part7 = both(1), both(7)
        for ch in range(CHUNKS):
            post(2, ch, part1[:, cols(ch)], chip(1))
            post(3, ch, part7[:, cols(ch)], chip(7))
        compute(0)
        join(2)
        acc[2] = both(2)
        acc[6] = both(6)
        for ch in range(CHUNKS):
            arrived(0, ch)
            arrived(6, ch)
            part = acc[2, :, cols(ch)] + msg_r[it, ch, 0].astype(F32)
            half = half_r[it, ch, 0].astype(F32)
            post(4, ch, jnp.concatenate([part[:, 0:HALF] + half, part[:, HALF:]], axis=1), chip(2))
            arrived(1, ch)
            arrived(7, ch)
            part = acc[6, :, cols(ch)] + msg_r[it, ch, 1].astype(F32)
            half = half_r[it, ch, 1].astype(F32)
            post(5, ch, jnp.concatenate([part[:, 0:HALF], part[:, HALF:] + half], axis=1), chip(6))
        join(3)
        acc[0] = both(0)
        for ch in range(CHUNKS):
            arrived(2, ch)
            arrived(3, ch)
            part = acc[0, :, cols(ch)] + msg_r[it, ch, 2].astype(F32) + msg_r[it, ch, 3].astype(F32)
            arrived(4, ch)
            arrived(5, ch)
            yield (part + msg_r[it, ch, 4].astype(F32) + msg_r[it, ch, 5].astype(F32)).astype(BF16)

    def gather(it, slot, pieces, use):
        here = c * 8
        there = (1 - c) * 8

        def pass_on(k, ch, d, dev, start=0, width=CW):
            ref = slot(here + (z + d) % 8, slice(ch * CW + start, ch * CW + start + width))
            send(ref, ref, ag_s.at[it, 1 if k in (4, 5) else 0], ag_r.at[it, ch, k], dev)

        def arrived(ch, k):
            wait(half_r.at[it, ch, 0] if k in (4, 5) else msg_r.at[it, ch, 0], ag_r.at[it, ch, k])

        def to_sibling(ch, d):
            ref = slot(here + (z + d) % 8, slice(ch * CW, (ch + 1) * CW))
            group = {0: 0, 6: 1, 2: 1, 7: 2, 1: 2, 5: 3, 3: 3, 4: 3}[d]
            send(ref, ref, sib_s.at[it], sib_r.at[it, ch, group], sibling)

        def use_own(ch, *ds):
            use([here + (z + d) % 8 for d in ds], slice(ch * CW, (ch + 1) * CW))

        def use_sibling(ch, *ds):
            group = {0: 0, 6: 1, 7: 2, 5: 3}[ds[0]]
            wait(msg_r.at[it, ch, 0:len(ds)], sib_r.at[it, ch, group])
            use([there + (z + d) % 8 for d in ds], slice(ch * CW, (ch + 1) * CW))

        for ch, piece in enumerate(pieces):
            slot(here + z, slice(ch * CW, (ch + 1) * CW))[...] = piece
            pass_on(0, ch, 0, chip(2))
            pass_on(1, ch, 0, chip(6))
            to_sibling(ch, 0)
        for ch in range(CHUNKS):
            pass_on(2, ch, 0, chip(1))
            pass_on(3, ch, 0, chip(7))
        use_own(0, 0)
        use_own(1, 0)
        use_sibling(0, 0)
        use_sibling(1, 0)
        for ch in range(CHUNKS):
            arrived(ch, 0)
            pass_on(4, ch, 6, chip(2), 0, HALF)
            pass_on(6, ch, 6, chip(1))
            to_sibling(ch, 6)
            arrived(ch, 1)
            pass_on(5, ch, 2, chip(6), HALF, HALF)
            pass_on(7, ch, 2, chip(7))
            to_sibling(ch, 2)
            use_own(ch, 6, 2)
        for ch in range(CHUNKS):
            arrived(ch, 2)
            to_sibling(ch, 7)
            arrived(ch, 3)
            to_sibling(ch, 1)
            use_own(ch, 7, 1)
            use_sibling(ch, 6, 2)
        use_sibling(0, 7, 1)
        use_sibling(1, 7, 1)
        for ch in range(CHUNKS):
            arrived(ch, 6)
            to_sibling(ch, 5)
            arrived(ch, 7)
            to_sibling(ch, 3)
            arrived(ch, 4)
            arrived(ch, 5)
            to_sibling(ch, 4)
            use_own(ch, 5, 3, 4)
        for ch in range(CHUNKS):
            use_sibling(ch, 5, 3, 4)

    qf[0] = jnp.zeros((K, WQ), F32)

    def use_first(ps, cols):
        qf[0] += sum(dot_nt(dv[p, NS:, cols], dv[p, :, cols]) for p in ps)

    gather(0, lambda p, cols: dv.at[p, NS:, cols], pull_and_scatter(0, projected), use_first)
    reduce_scatter_q(1, qf[0])
    exchange_gram(0, qf[0, :, NS:])
    gather_q(1)
    inv = inverse_factor(join_gram(0))
    projected = dot_exact(inv, join_q(1)).astype(BF16)

    qf[1] = jnp.zeros((K, WQ), F32)

    g2[...] = jnp.zeros((K, K), F32)

    def use_second(ps, cols):
        qf[1, :, 0:NS] += sum(dot_nt(x2[p, :, cols], dv[p, 0:NS, cols]) for p in ps)
        g2[...] += sum(dot_nt(x2[p, :, cols], x2[p, :, cols]) for p in ps)

    gather(1, lambda p, cols: x2.at[p, :, cols], pull_and_scatter(1, projected), use_second)
    exchange_gram(1, g2[...])
    for p in range(NP):
        pltpu.make_async_copy(x2.at[p], x2_out.at[:, p * PW:(p + 1) * PW], o_sem).start()

    along = qf[1, :, 0:NS]
    cs[0:K // 2, :] = pack(lax.dot_general(along, along, (((1,), (1,)), ((), ())), preferred_element_type=F32,
                                           precision=lax.Precision.HIGHEST))
    send(cs, cr, c_s.at[0], c_r.at[0], sibling)
    wait(cr, c_r.at[0])
    cg[0] = cs[...] + cr[...]
    for d in COLUMN:
        send(cg.at[0], cg.at[d], c_s.at[1], c_r.at[1], chip(d))

    wait(gg.at[0, 1:16], g_s.at[0])
    wait(qs.at[1, 1:16], ar_s.at[0, 1])
    wait(qs.at[1, 1:16], ar_s.at[1, 1])
    wait(cs, c_s.at[0])
    for it in range(2):
        wait(psend.at[it], pair_s.at[it])
        wait(msg_s.at[it], rs_s.at[it, 0])
        wait(half_s.at[it], rs_s.at[it, 1])
        wait(msg_s.at[it], ag_s.at[it, 0])
        wait(half_s.at[it], ag_s.at[it, 1])
        wait(psend.at[it], sib_s.at[it])

    inv = inverse_factor(join_gram(1))
    factor_ref[...] = inv * math.sqrt(FEATURES)
    wait(cg.at[1:8], c_r.at[1])
    total = cg[z]
    for j in range(1, 8):
        total = total + cg[(z - j + 8) % 8]
    spread = dot_exact(inv, unpack(total[0:K // 2])) * inv
    captured = lax.dot_general(jnp.ones((8, K), F32), spread, (((1,), (1,)), ((), ())),
                               preferred_element_type=F32, precision=lax.Precision.HIGHEST)
    score_ref[...] = FEATURES * captured[0:1, :] / (total[K // 2:K // 2 + 1, 0:K] + 1e-6)
    wait(gg.at[1, 1:16], g_s.at[1])
    wait(cg.at[1:8], c_s.at[1])
    wait(x2_out, o_sem)


def on_device(differences, start_block):
    dma = pltpu.SemaphoreType.DMA
    pulled, factor, scores = pl.pallas_call(
        kernel,
        out_shape=(jax.ShapeDtypeStruct((K, WF), BF16), jax.ShapeDtypeStruct((K, K), F32),
                   jax.ShapeDtypeStruct((1, K), F32)),
        in_specs=[pl.BlockSpec(memory_space=pltpu.HBM), pl.BlockSpec(memory_space=pltpu.HBM)],
        out_specs=(pl.BlockSpec(memory_space=pltpu.HBM), pl.BlockSpec(memory_space=pltpu.VMEM),
                   pl.BlockSpec(memory_space=pltpu.VMEM)),
        scratch_shapes=[
            pltpu.VMEM((NP, WQ, PW), BF16),
            pltpu.VMEM((NP, K, PW), BF16),
            pltpu.VMEM((NP, K, PW), BF16),
            pltpu.VMEM((2, 8, K, PW), BF16),
            pltpu.VMEM((2, 8, K, PW), BF16),
            pltpu.VMEM((2, CHUNKS, 6, K, CW), BF16),
            pltpu.VMEM((2, CHUNKS, 6, K, CW), BF16),
            pltpu.VMEM((2, CHUNKS, 2, K, HALF), BF16),
            pltpu.VMEM((2, CHUNKS, 2, K, HALF), BF16),
            pltpu.VMEM((8, K, PW), F32),
            pltpu.VMEM((2, 16, ROWS, WQ), F32),
            pltpu.VMEM((2, 16, ROWS, WQ), F32),
            pltpu.VMEM((2, ROWS, WQ), F32),
            pltpu.VMEM((2, 16, ROWS, WQ), F32),
            pltpu.VMEM((4, K, WQ), F32),
            pltpu.VMEM((2, 16, K // 2, 128), F32),
            pltpu.VMEM((K // 2 + 8, 128), F32),
            pltpu.VMEM((K // 2 + 8, 128), F32),
            pltpu.VMEM((8, K // 2 + 8, 128), F32),
            pltpu.VMEM((K, K), F32),
            dma((NP // LOAD,)), dma, dma,
            dma((2, 2)), dma((2, 2)),
            dma((2,)), dma((2, 4)),
            dma((2, 2)), dma((2, CHUNKS, 8)),
            dma((2, 2)), dma((2, CHUNKS, 8)),
            dma((2,)), dma((2, CHUNKS, 4)),
            dma((2,)), dma((2,)),
            dma((2,)), dma((2,)),
        ],
        compiler_params=pltpu.CompilerParams(collective_id=0, has_side_effects=True, vmem_limit_bytes=56 * 1024 * 1024),
    )(differences, start_block)
    directions = jnp.dot(factor, pulled.astype(F32), precision=lax.Precision.HIGH)
    return directions, scores


def solution(mesh):
    in_specs = (P("samp", "feat"), P(None, "feat"))
    out_specs = (P(None, "feat"), P("feat", None))
    return jax.shard_map(
        on_device, mesh=mesh, in_specs=in_specs, out_specs=out_specs, check_vma=False
    )
```

time: 95.9 us -> 93.2 us (0.972)
  Pallas kernels: 94.9 us -> 88.7 us
  matrix products: 0 us -> 3.26 us
    pallas_call x2 -> x1, Pallas kernels: 94.9 us -> 88.7 us  [on_device(): pl.pallas_call(kernel, out_shape=(jax.ShapeDtypeStruct((K, WF), BF16), ja...]
    dot_general x0 -> x1, matrix products: none -> 3.26 us  [on_device(): jnp.dot(factor, pulled.astype(F32), precision=lax.Precision.HIGH)]
where the time goes in v5:
time: 93.2 us; the launch traced here: 93.1 us
  Pallas kernels  88.7 us (95%)
  matrix products  3.26 us (3%)
    pallas_call x1, Pallas kernels, on_device(): pl.pallas_call(kernel, out_shape=(jax.ShapeDtypeStruct((K, WF), BF16), ja...  88.7 us
    dot_general x1, matrix products, on_device(): jnp.dot(factor, pulled.astype(F32), precision=lax.Precision.HIGH)  3.26 us

profile of v5, /device:TPU:1, one launch (start us, length us, event | category | flops | bytes accessed | tf_op | source)
XLA Modules:
  0.0 93.1 jit_solution(5293656527242703748)
XLA Ops:
  0.6 88.7 %shard_map.41 = (bf16[64,8192]{1,0:T(8,128)(2,1)}, f32[64,64]{1,0:T(8,128)}, f32[1,64]{1,0:T(1,128)}) custom-call(bf16[576,8192]{1,0:T(8,128)(2,1)} %d_hbm.1, bf16[64,8192]{1,0:T(8,128)(2,1)} %s_hbm.1), custom_call_target="tpu_custom_call" | custom-call | tf_op jit(solution)/shard_map/pallas_call | solution.py:384
  89.3 0.0 copy-start
  89.3 3.3 %fusion = f32[64,8192]{1,0:T(8,128)} fusion(f32[64,64]{1,0:T(8,128)} %get-tuple-element.5, bf16[64,8192]{1,0:T(8,128)(2,1)} %get-tuple-element.6), kind=kOutput, calls=%fused_computation | convolution fusion | flops 201326592 | bytes 3162112 | tf_op jit(solution)/shard_map/dot_general | solution.py:423
  92.6 0.0 copy-done
  92.6 0.5 copy.5
Async XLA Ops:
  89.3 3.3 %copy-start = (f32[1,64]{1,0:T(1,128)S(1)}, f32[1,64]{1,0:T(1,128)}, u32[]{:S(2)}) copy-start(f32[1,64]{1,0:T(1,128)} %get-tuple-element.11) | copy-start | bytes 772

commit v6 on v5

--- a/solution.py
+++ b/solution.py
@@ -9,6 +9,7 @@
 
 FEATURES = 131072
 K = 64
+H = K // 2
 NS = 576
 WF = 8192
 NP = 16
@@ -85,7 +86,7 @@
 
 def kernel(d_hbm, s_hbm, x2_out, factor_ref, score_ref,
            dv, sv, x2, psend, precv, msg_s, msg_r, half_s, half_r, acc,
-           qs, qr, qo, qg, qf, gg, cs, cr, cg, g2,
+           qs, qr, qo, qg, qf, gg, cs, cr, cg, g2, keep,
            d_sem, s_sem, o_sem, ar_s, ar_r, pair_s, pair_r, rs_s, rs_r,
            ag_s, ag_r, sib_s, sib_r, g_s, g_r, c_s, c_r):
     samp = lax.axis_index("samp")
@@ -172,7 +173,7 @@
         return total + jnp.sum(wide * wide, axis=0, keepdims=True)
 
     energy = lax.fori_loop(0, NP, energy_step, jnp.zeros((1, PW), F32))
-    cs[K // 2:, :] = jnp.broadcast_to(jnp.sum(energy, axis=1, keepdims=True), (8, 128))
+    keep[...] = jnp.broadcast_to(jnp.sum(energy, axis=1, keepdims=True), (8, 128))
     gather_q(0)
     projected = join_q(0).astype(BF16)
 
@@ -344,8 +345,15 @@
         pltpu.make_async_copy(x2.at[p], x2_out.at[:, p * PW:(p + 1) * PW], o_sem).start()
 
     along = qf[1, :, 0:NS]
-    cs[0:K // 2, :] = pack(lax.dot_general(along, along, (((1,), (1,)), ((), ())), preferred_element_type=F32,
-                                           precision=lax.Precision.HIGHEST))
+    high = along.astype(BF16)
+    rest = along - high.astype(F32)
+    middle = rest.astype(BF16)
+    low = (rest - middle.astype(F32)).astype(BF16)
+    parts = jnp.concatenate([high, middle, low], axis=0)
+    nine = dot_nt(parts, parts)
+    rows = nine[0:K] + nine[K:2 * K] + nine[2 * K:]
+    square = rows[:, 0:K] + rows[:, K:2 * K] + rows[:, 2 * K:]
+    cs[...] = jnp.concatenate([square[0:H, :], square[H:, H:], jnp.broadcast_to(keep[0:1, 0:H], (H, H))], axis=1)
     send(cs, cr, c_s.at[0], c_r.at[0], sibling)
     wait(cr, c_r.at[0])
     cg[0] = cs[...] + cr[...]
@@ -370,10 +378,13 @@
     total = cg[z]
     for j in range(1, 8):
         total = total + cg[(z - j + 8) % 8]
-    spread = dot_exact(inv, unpack(total[0:K // 2])) * inv
+    once = lax.broadcasted_iota(jnp.int32, (H, K), 1) < H
+    form = jnp.concatenate([jnp.where(once, total[:, 0:K], 2.0 * total[:, 0:K]),
+                            jnp.concatenate([jnp.zeros((H, H), F32), total[:, K:K + H]], axis=1)], axis=0)
+    spread = dot_exact(inv, form) * inv
     captured = lax.dot_general(jnp.ones((8, K), F32), spread, (((1,), (1,)), ((), ())),
                                preferred_element_type=F32, precision=lax.Precision.HIGHEST)
-    score_ref[...] = FEATURES * captured[0:1, :] / (total[K // 2:K // 2 + 1, 0:K] + 1e-6)
+    score_ref[...] = FEATURES * captured[0:1, :] / (total[0:1, K + H:K + H + 1] + 1e-6)
     wait(gg.at[1, 1:16], g_s.at[1])
     wait(cg.at[1:8], c_s.at[1])
     wait(x2_out, o_sem)
@@ -405,10 +416,11 @@
             pltpu.VMEM((2, 16, ROWS, WQ), F32),
             pltpu.VMEM((4, K, WQ), F32),
             pltpu.VMEM((2, 16, K // 2, 128), F32),
-            pltpu.VMEM((K // 2 + 8, 128), F32),
-            pltpu.VMEM((K // 2 + 8, 128), F32),
-            pltpu.VMEM((8, K // 2 + 8, 128), F32),
+            pltpu.VMEM((H, 128), F32),
+            pltpu.VMEM((H, 128), F32),
+            pltpu.VMEM((8, H, 128), F32),
             pltpu.VMEM((K, K), F32),
+            pltpu.VMEM((8, 128), F32),
             dma((NP // LOAD,)), dma, dma,
             dma((2, 2)), dma((2, 2)),
             dma((2,)), dma((2, 4)),
@@ -418,7 +430,7 @@
             dma((2,)), dma((2,)),
             dma((2,)), dma((2,)),
         ],
-        compiler_params=pltpu.CompilerParams(collective_id=0, has_side_effects=True, vmem_limit_bytes=56 * 1024 * 1024),
+        compiler_params=pltpu.CompilerParams(collective_id=0, has_side_effects=True, vmem_limit_bytes=52 * 1024 * 1024),
     )(differences, start_block)
     directions = jnp.dot(factor, pulled.astype(F32), precision=lax.Precision.HIGH)
     return directions, scores

time: 93.2 us -> 90.8 us (0.974)
  matrix products: 3.26 us -> 2.01 us
  Pallas kernels: 88.7 us -> 87.6 us
    dot_general x1, matrix products: 3.26 us -> 2.01 us  [on_device(): jnp.dot(factor, pulled.astype(F32), precision=lax.Precision.HIGH)]
    pallas_call x1, Pallas kernels: 88.7 us -> 87.6 us  [on_device(): pl.pallas_call(kernel, out_shape=(jax.ShapeDtypeStruct((K, WF), BF16), ja...]
where the time goes in v6:
time: 90.8 us; the launch traced here: 90.7 us
  Pallas kernels  87.6 us (96%)
  matrix products  2.01 us (2%)
    pallas_call x1, Pallas kernels, on_device(): pl.pallas_call(kernel, out_shape=(jax.ShapeDtypeStruct((K, WF), BF16), ja...  87.6 us
    dot_general x1, matrix products, on_device(): jnp.dot(factor, pulled.astype(F32), precision=lax.Precision.HIGH)  2.01 us

profile of v6, /device:TPU:1, one launch (start us, length us, event | category | flops | bytes accessed | tf_op | source)
XLA Modules:
  0.0 90.7 jit_solution(671327945791563522)
XLA Ops:
  0.6 87.6 %shard_map.41 = (bf16[64,8192]{1,0:T(8,128)(2,1)S(1)}, f32[64,64]{1,0:T(8,128)S(1)}, f32[1,64]{1,0:T(1,128)S(1)}) custom-call(bf16[576,8192]{1,0:T(8,128)(2,1)} %d_hbm.1, bf16[64,8192]{1,0:T(8,128)(2,1)} %s_hbm.1), custom_call_target="tpu_custom_call" | custom-call | tf_op jit(solution)/shard_map/pallas_call | solution.py:395
  88.2 2.0 %fusion = f32[64,8192]{1,0:T(8,128)} fusion(f32[64,64]{1,0:T(8,128)S(1)} %get-tuple-element.5, bf16[64,8192]{1,0:T(8,128)(2,1)S(1)} %get-tuple-element.6), kind=kOutput, calls=%fused_computation | convolution fusion | flops 201326592 | bytes 3162112 | tf_op jit(solution)/shard_map/dot_general | solution.py:435
  90.2 0.5 copy.5

commit v7 on v6

--- a/solution.py
+++ b/solution.py
@@ -178,16 +178,18 @@
     projected = join_q(0).astype(BF16)
 
     def pull_and_scatter(it, projected):
-        def compute(d):
-            there = (z + d) % 8
-            k = PAIRS.index(d)
-            psend[it, k] = dot_nn(projected, dv[(1 - c) * 8 + there, 0:NS, :]).astype(BF16)
-            group = 0 if k < 3 else 1 if k < 5 else 2 if k < 7 else 3
-            send(psend.at[it, k], precv.at[it, k], pair_s.at[it], pair_r.at[it, group], sibling)
-            acc[d] = dot_nn(projected, dv[c * 8 + there, 0:NS, :])
+        def theirs(*ds):
+            for d in ds:
+                k = PAIRS.index(d)
+                psend[it, k] = dot_nn(projected, dv[(1 - c) * 8 + (z + d) % 8, 0:NS, :]).astype(BF16)
+                send(psend.at[it, k], precv.at[it, k], pair_s.at[it], pair_r.at[it, (k + 1) // 2], sibling)
+
+        def ours(*ds):
+            for d in ds:
+                acc[d] = dot_nn(projected, dv[c * 8 + (z + d) % 8, 0:NS, :])
 
         def join(group):
-            first, last = ((0, 3), (3, 5), (5, 7), (7, 8))[group]
+            first, last = ((0, 1), (1, 3), (3, 5), (5, 7), (7, 8))[group]
             wait(precv.at[it, first:last], pair_r.at[it, group])
 
         def both(d):
@@ -207,28 +209,29 @@
         def cols(ch):
             return slice(ch * CW, (ch + 1) * CW)
 
-        compute(4)
-        compute(3)
-        compute(5)
-        compute(2)
+        theirs(4, 3, 5)
+        ours(4, 3, 5)
+        theirs(1, 7)
         join(0)
-        part4, part3, part5 = both(4), both(3), both(5)
+        part4 = both(4)
         for ch in range(CHUNKS):
             part = part4[:, cols(ch)]
             post_half(0, ch, part[:, 0:HALF], chip(2))
             post_half(1, ch, part[:, HALF:], chip(6))
+        join(1)
+        part3, part5 = both(3), both(5)
+        for ch in range(CHUNKS):
             post(0, ch, part3[:, cols(ch)], chip(1))
             post(1, ch, part5[:, cols(ch)], chip(7))
-        compute(6)
-        compute(1)
-        compute(7)
-        join(1)
+        ours(1, 7)
+        theirs(2, 6, 0)
+        join(2)
         part1, part7 = both(1), both(7)
         for ch in range(CHUNKS):
             post(2, ch, part1[:, cols(ch)], chip(1))
             post(3, ch, part7[:, cols(ch)], chip(7))
-        compute(0)
-        join(2)
+        ours(2, 6, 0)
+        join(3)
         acc[2] = both(2)
         acc[6] = both(6)
         for ch in range(CHUNKS):
@@ -242,7 +245,7 @@
             part = acc[6, :, cols(ch)] + msg_r[it, ch, 1].astype(F32)
             half = half_r[it, ch, 1].astype(F32)
             post(5, ch, jnp.concatenate([part[:, 0:HALF], part[:, HALF:] + half], axis=1), chip(6))
-        join(3)
+        join(4)
         acc[0] = both(0)
         for ch in range(CHUNKS):
             arrived(2, ch)
@@ -423,7 +426,7 @@
             pltpu.VMEM((8, 128), F32),
             dma((NP // LOAD,)), dma, dma,
             dma((2, 2)), dma((2, 2)),
-            dma((2,)), dma((2, 4)),
+            dma((2,)), dma((2, 5)),
             dma((2, 2)), dma((2, CHUNKS, 8)),
             dma((2, 2)), dma((2, CHUNKS, 8)),
             dma((2,)), dma((2, CHUNKS, 4)),

time: 90.8 us -> 89.7 us (0.988)
  Pallas kernels: 87.6 us -> 86.5 us
    pallas_call x1, Pallas kernels: 87.6 us -> 86.5 us  [on_device(): pl.pallas_call(kernel, out_shape=(jax.ShapeDtypeStruct((K, WF), BF16), ja...]
where the time goes in v7:
time: 89.7 us; the launch traced here: 89.6 us
  Pallas kernels  86.5 us (96%)
  matrix products  2.01 us (2%)
    pallas_call x1, Pallas kernels, on_device(): pl.pallas_call(kernel, out_shape=(jax.ShapeDtypeStruct((K, WF), BF16), ja...  86.5 us
    dot_general x1, matrix products, on_device(): jnp.dot(factor, pulled.astype(F32), precision=lax.Precision.HIGH)  2.01 us

profile of v7, /device:TPU:1, one launch (start us, length us, event | category | flops | bytes accessed | tf_op | source)
XLA Modules:
  0.0 89.6 jit_solution(9073544255987470748)
XLA Ops:
  0.6 86.5 %shard_map.41 = (bf16[64,8192]{1,0:T(8,128)(2,1)S(1)}, f32[64,64]{1,0:T(8,128)S(1)}, f32[1,64]{1,0:T(1,128)S(1)}) custom-call(bf16[576,8192]{1,0:T(8,128)(2,1)} %d_hbm.1, bf16[64,8192]{1,0:T(8,128)(2,1)} %s_hbm.1), custom_call_target="tpu_custom_call" | custom-call | tf_op jit(solution)/shard_map/pallas_call | solution.py:398
  87.1 2.0 %fusion = f32[64,8192]{1,0:T(8,128)} fusion(f32[64,64]{1,0:T(8,128)S(1)} %get-tuple-element.5, bf16[64,8192]{1,0:T(8,128)(2,1)S(1)} %get-tuple-element.6), kind=kOutput, calls=%fused_computation | convolution fusion | flops 201326592 | bytes 3162112 | tf_op jit(solution)/shard_map/dot_general | solution.py:438
  89.1 0.5 copy.5

commit v8 on v7

--- a/solution.py
+++ b/solution.py
@@ -19,7 +19,7 @@
 HALF = CW // 2
 ROWS = K // 16
 WQ = NS + K
-LOAD = 4
+LOAD = 1
 MESH = pl.DeviceIdType.MESH
 F32 = jnp.float32
 BF16 = jnp.bfloat16

time: 89.7 us -> 90.3 us (level)
  no operation moved by 1% of the time
where the time goes in v8:
time: 90.3 us; the launch traced here: 90.2 us
  Pallas kernels  87.1 us (96%)
  matrix products  2.01 us (2%)
    pallas_call x1, Pallas kernels, on_device(): pl.pallas_call(kernel, out_shape=(jax.ShapeDtypeStruct((K, WF), BF16), ja...  87.1 us
    dot_general x1, matrix products, on_device(): jnp.dot(factor, pulled.astype(F32), precision=lax.Precision.HIGH)  2.01 us

profile of v8, /device:TPU:1, one launch (start us, length us, event | category | flops | bytes accessed | tf_op | source)
XLA Modules:
  0.0 90.2 jit_solution(2840850494020701700)
XLA Ops:
  0.6 87.1 %shard_map.41 = (bf16[64,8192]{1,0:T(8,128)(2,1)S(1)}, f32[64,64]{1,0:T(8,128)S(1)}, f32[1,64]{1,0:T(1,128)S(1)}) custom-call(bf16[576,8192]{1,0:T(8,128)(2,1)} %d_hbm.1, bf16[64,8192]{1,0:T(8,128)(2,1)} %s_hbm.1), custom_call_target="tpu_custom_call" | custom-call | tf_op jit(solution)/shard_map/pallas_call | solution.py:398
  87.7 2.0 %fusion = f32[64,8192]{1,0:T(8,128)} fusion(f32[64,64]{1,0:T(8,128)S(1)} %get-tuple-element.5, bf16[64,8192]{1,0:T(8,128)(2,1)S(1)} %get-tuple-element.6), kind=kOutput, calls=%fused_computation | convolution fusion | flops 201326592 | bytes 3162112 | tf_op jit(solution)/shard_map/dot_general | solution.py:438
  89.7 0.5 copy.5
